TPU v7x, 128 devices: a whole 4x4x4 slice. The times are simulated.
128 devices in a mesh: row: 32 (over y, z, core), col: 4 (over x).
Axes of the slice: x: 4, y: 4, z: 4, core: 2. Of those that a mesh axis runs over, the one named last changes fastest.
Arguments:
- disk: bfloat16 [16, 4096, 2048], P(None, 'row', 'col'), may hold values from -6 to 6
- response: bfloat16 [19, 19], replicated, may hold values from -0.3125 to 0.3125
- spectra: bfloat16 [2048, 196608], P('col', 'row'), may hold values from -6 to 6
- srf: bfloat16 [16, 2048], P(None, 'col'), may hold values from -0.125 to 0.125
- send_pix: int32 [4718592], P(('row', 'col')), may hold values from 0 to 65535, as said below
- recv_foot: int32 [4718592], P(('row', 'col')), may hold values from 0 to 1536, as said below
Outputs:
- blurred: bfloat16 [16, 4096, 2048], P(None, 'row', 'col')
- mismatch: float32 [16, 196608], P(None, ('row', 'col'))
Inputs may be any that keep to these rules, and one draw needn't show every extreme that they name: `send_pix`: every value is a local pixel offset in the sending tile, row * 512 + column. `recv_foot`: within each receiving device's 128 * 288 slots, every one of its 1536 footprints is named exactly 16 times; 1536 marks a slot that carries nothing; for each receiving device some sending tile fills all 288 of its slots.
All inputs are finite; a program needn't handle non-finite values.
Results may differ from a plain program's by a relative error of at most 0.001.
Values may be sent and summed in bfloat16 or wider, within the bound.
A program may use at most 128 MiB of HBM per device.

v0:
```python
import jax
import jax.numpy as jnp
from jax import lax
from jax.sharding import PartitionSpec as P

NSAMP = 16


def with_halo(cells, sides, width):
    for axis, dim in sides:
        count = lax.axis_size(axis)
        ends = count - 1
        head = lax.slice_in_dim(cells, 0, width, axis=dim)
        tail = lax.slice_in_dim(cells, cells.shape[dim] - width, cells.shape[dim], axis=dim)
        cells = jnp.concatenate(
            [
                lax.ppermute(tail, axis, [(i, (i + 1) % count) for i in range(ends)]),
                cells,
                lax.ppermute(head, axis, [((i + 1) % count, i) for i in range(ends)]),
            ],
            axis=dim,
        )
    return cells


def body(disk, response, spectra, srf, send_pix, recv_foot):
    band_count, tile_rows, tile_cols = disk.shape
    stencil = response.shape[0]
    margin = stencil // 2
    padded = with_halo(disk, (("row", 1), ("col", 2)), margin)
    lane_width = 128
    window = lane_width + stencil - 1
    column_blocks = tile_cols // lane_width
    stacked = jnp.stack(
        [
            lax.slice_in_dim(
                padded, start_col * lane_width, start_col * lane_width + window, axis=2
            )
            for start_col in range(column_blocks)
        ],
        axis=2,
    )
    shifts = jnp.arange(window)[:, None] - jnp.arange(lane_width)[None, :]
    picker = (shifts[None, :, :] == jnp.arange(stencil)[:, None, None]).astype(jnp.float32)
    banded = jnp.einsum("ac,cwo->awo", response.astype(jnp.float32), picker).astype(jnp.bfloat16)

    def add_offset(offset_row, running):
        taken = lax.dynamic_slice_in_dim(stacked, offset_row, tile_rows, axis=1)
        return running + jnp.dot(
            taken.reshape(-1, window), banded[offset_row], preferred_element_type=jnp.float32
        )

    running = lax.fori_loop(
        0,
        stencil,
        add_offset,
        jnp.zeros((band_count * tile_rows * column_blocks, lane_width), jnp.float32),
    )
    blurred = running.reshape(band_count, tile_rows, tile_cols).astype(jnp.bfloat16)
    flat_tile = blurred.reshape(band_count, tile_rows * tile_cols)
    outgoing = jnp.take(flat_tile, send_pix, axis=1)
    incoming = lax.all_to_all(outgoing, ("row", "col"), split_axis=1, concat_axis=1, tiled=True)
    col_count = lax.axis_size("col")
    footprints = spectra.shape[1] // col_count
    lo_width = min(128, footprints)
    hi_count = footprints // lo_width
    low_part = recv_foot % lo_width
    high_part = recv_foot // lo_width
    low_table = (low_part[:, None] == jnp.arange(lo_width, dtype=jnp.int32)[None, :]).astype(
        jnp.bfloat16
    )
    high_table = (high_part[None, :] == jnp.arange(hi_count, dtype=jnp.int32)[:, None]).astype(
        jnp.bfloat16
    )
    masked = (incoming[:, None, :] * high_table[None, :, :]).reshape(band_count * hi_count, -1)
    totals = jnp.dot(masked, low_table, preferred_element_type=jnp.float32)
    imager = totals.reshape(band_count, footprints) / NSAMP
    partial_bands = jnp.dot(srf, spectra, preferred_element_type=jnp.float32)
    evolved = lax.psum_scatter(partial_bands, "col", scatter_dimension=1, tiled=True)
    return (blurred, evolved - imager)


def solution(mesh):
    placed = (
        P(None, "row", "col"),
        P(),
        P("col", "row"),
        P(None, "col"),
        P(("row", "col")),
        P(("row", "col")),
    )
    return jax.shard_map(
        body,
        mesh=mesh,
        in_specs=placed,
        out_specs=(P(None, "row", "col"), P(None, ("row", "col"))),
        check_vma=False,
    )
```

profile of v0, /device:TPU:1, one launch (start us, length us, event | category | flops | bytes accessed | tf_op | source)
XLA Modules:
  0.0 699.5 jit_solution(2342505392806789030)
XLA Ops:
  8.4 4.9 collective-permute-start
  15.6 4.5 fusion.19
  48.1 397.4 %while.14 = (s32[]{:T(128)}, f32[8192,128]{1,0:T(8,128)}, bf16[16,146,4,146]{3,0,2,1:T(8,128)(2,1)}, bf16[19,146,128]{2,1,0:T(8,128)(2,1)}, s32[]{:T(128)}, /*index=5*/s32[]{:T(128)}) while((s32[]{:T(128)}, f32[8192,128]{1,0:T(8,128)}, bf16[16,146,4,146]{3,0,2,1:T(8,128)(2,1)}, bf16[19,146,128]{2,1,0:T(8,128)(2,1)}, s32[]{:T(128)}, ...), condition=%wide.region_1.0_spmd.clone, body=%wide.region_0.0_spmd.clone.sunk | while | flops 308281344 | bytes 26974804 | solution.py:53
  50.7 4.1 copy.54
  54.8 7.6 %reshape.85 = bf16[8192,146]{1,0:T(8,128)(2,1)} reshape(bf16[16,128,4,146]{3,2,1,0:T(4,128)(2,1)} %copy.54) | data formatting | bytes 4784128 | tf_op jit(solution)/shard_map/while/body/eval_jaxpr/reshape | solution.py:50
  62.4 5.4 convolution_add_fusion.2
  70.3 4.1 copy.54
  74.4 7.6 %reshape.85 = bf16[8192,146]{1,0:T(8,128)(2,1)} reshape(bf16[16,128,4,146]{3,2,1,0:T(4,128)(2,1)} %copy.54) | data formatting | bytes 4784128 | tf_op jit(solution)/shard_map/while/body/eval_jaxpr/reshape | solution.py:50
  82.1 6.7 convolution_add_fusion.2
  91.3 4.1 copy.54
  95.4 7.6 %reshape.85 = bf16[8192,146]{1,0:T(8,128)(2,1)} reshape(bf16[16,128,4,146]{3,2,1,0:T(4,128)(2,1)} %copy.54) | data formatting | bytes 4784128 | tf_op jit(solution)/shard_map/while/body/eval_jaxpr/reshape | solution.py:50
  103.0 6.7 convolution_add_fusion.2
  112.3 4.1 copy.54
  116.4 7.6 %reshape.85 = bf16[8192,146]{1,0:T(8,128)(2,1)} reshape(bf16[16,128,4,146]{3,2,1,0:T(4,128)(2,1)} %copy.54) | data formatting | bytes 4784128 | tf_op jit(solution)/shard_map/while/body/eval_jaxpr/reshape | solution.py:50
  124.0 6.7 convolution_add_fusion.2
  133.3 4.1 copy.54
  137.4 7.6 %reshape.85 = bf16[8192,146]{1,0:T(8,128)(2,1)} reshape(bf16[16,128,4,146]{3,2,1,0:T(4,128)(2,1)} %copy.54) | data formatting | bytes 4784128 | tf_op jit(solution)/shard_map/while/body/eval_jaxpr/reshape | solution.py:50
  145.0 6.7 convolution_add_fusion.2
  154.3 4.1 copy.54
  158.4 7.6 %reshape.85 = bf16[8192,146]{1,0:T(8,128)(2,1)} reshape(bf16[16,128,4,146]{3,2,1,0:T(4,128)(2,1)} %copy.54) | data formatting | bytes 4784128 | tf_op jit(solution)/shard_map/while/body/eval_jaxpr/reshape | solution.py:50
  166.0 6.7 convolution_add_fusion.2
  175.3 4.1 copy.54
  179.4 7.6 %reshape.85 = bf16[8192,146]{1,0:T(8,128)(2,1)} reshape(bf16[16,128,4,146]{3,2,1,0:T(4,128)(2,1)} %copy.54) | data formatting | bytes 4784128 | tf_op jit(solution)/shard_map/while/body/eval_jaxpr/reshape | solution.py:50
  187.0 6.7 convolution_add_fusion.2
  196.2 4.1 copy.54
  200.3 7.6 %reshape.85 = bf16[8192,146]{1,0:T(8,128)(2,1)} reshape(bf16[16,128,4,146]{3,2,1,0:T(4,128)(2,1)} %copy.54) | data formatting | bytes 4784128 | tf_op jit(solution)/shard_map/while/body/eval_jaxpr/reshape | solution.py:50
  208.0 6.7 convolution_add_fusion.2
  217.2 4.1 copy.54
  221.3 7.6 %reshape.85 = bf16[8192,146]{1,0:T(8,128)(2,1)} reshape(bf16[16,128,4,146]{3,2,1,0:T(4,128)(2,1)} %copy.54) | data formatting | bytes 4784128 | tf_op jit(solution)/shard_map/while/body/eval_jaxpr/reshape | solution.py:50
  228.9 6.7 convolution_add_fusion.2
  238.2 4.1 copy.54
  242.3 7.6 %reshape.85 = bf16[8192,146]{1,0:T(8,128)(2,1)} reshape(bf16[16,128,4,146]{3,2,1,0:T(4,128)(2,1)} %copy.54) | data formatting | bytes 4784128 | tf_op jit(solution)/shard_map/while/body/eval_jaxpr/reshape | solution.py:50
  249.9 6.7 convolution_add_fusion.2
  259.2 4.1 copy.54
  263.3 7.6 %reshape.85 = bf16[8192,146]{1,0:T(8,128)(2,1)} reshape(bf16[16,128,4,146]{3,2,1,0:T(4,128)(2,1)} %copy.54) | data formatting | bytes 4784128 | tf_op jit(solution)/shard_map/while/body/eval_jaxpr/reshape | solution.py:50
  270.9 6.7 convolution_add_fusion.2
  280.2 4.1 copy.54
  284.3 7.6 %reshape.85 = bf16[8192,146]{1,0:T(8,128)(2,1)} reshape(bf16[16,128,4,146]{3,2,1,0:T(4,128)(2,1)} %copy.54) | data formatting | bytes 4784128 | tf_op jit(solution)/shard_map/while/body/eval_jaxpr/reshape | solution.py:50
  291.9 6.7 convolution_add_fusion.2
  301.2 4.1 copy.54
  305.3 7.6 %reshape.85 = bf16[8192,146]{1,0:T(8,128)(2,1)} reshape(bf16[16,128,4,146]{3,2,1,0:T(4,128)(2,1)} %copy.54) | data formatting | bytes 4784128 | tf_op jit(solution)/shard_map/while/body/eval_jaxpr/reshape | solution.py:50
  312.9 6.7 convolution_add_fusion.2
  322.2 4.1 copy.54
  326.3 7.6 %reshape.85 = bf16[8192,146]{1,0:T(8,128)(2,1)} reshape(bf16[16,128,4,146]{3,2,1,0:T(4,128)(2,1)} %copy.54) | data formatting | bytes 4784128 | tf_op jit(solution)/shard_map/while/body/eval_jaxpr/reshape | solution.py:50
  333.9 6.7 convolution_add_fusion.2
  343.1 4.1 copy.54
  347.2 7.6 %reshape.85 = bf16[8192,146]{1,0:T(8,128)(2,1)} reshape(bf16[16,128,4,146]{3,2,1,0:T(4,128)(2,1)} %copy.54) | data formatting | bytes 4784128 | tf_op jit(solution)/shard_map/while/body/eval_jaxpr/reshape | solution.py:50
  354.8 6.7 convolution_add_fusion.2
  368.2 7.6 %reshape.85 = bf16[8192,146]{1,0:T(8,128)(2,1)} reshape(bf16[16,128,4,146]{3,2,1,0:T(4,128)(2,1)} %copy.54) | data formatting | bytes 4784128 | tf_op jit(solution)/shard_map/while/body/eval_jaxpr/reshape | solution.py:50
  375.8 6.7 convolution_add_fusion.2
  389.2 7.6 %reshape.85 = bf16[8192,146]{1,0:T(8,128)(2,1)} reshape(bf16[16,128,4,146]{3,2,1,0:T(4,128)(2,1)} %copy.54) | data formatting | bytes 4784128 | tf_op jit(solution)/shard_map/while/body/eval_jaxpr/reshape | solution.py:50
  396.8 6.7 convolution_add_fusion.2
  410.2 7.6 %reshape.85 = bf16[8192,146]{1,0:T(8,128)(2,1)} reshape(bf16[16,128,4,146]{3,2,1,0:T(4,128)(2,1)} %copy.54) | data formatting | bytes 4784128 | tf_op jit(solution)/shard_map/while/body/eval_jaxpr/reshape | solution.py:50
  417.8 6.7 convolution_add_fusion.2
  431.2 7.6 %reshape.85 = bf16[8192,146]{1,0:T(8,128)(2,1)} reshape(bf16[16,128,4,146]{3,2,1,0:T(4,128)(2,1)} %copy.54) | data formatting | bytes 4784128 | tf_op jit(solution)/shard_map/while/body/eval_jaxpr/reshape | solution.py:50
  438.8 6.7 convolution_add_fusion.2
  449.8 12.4 %copy.46 = bf16[16,65536]{0,1:T(8,128)(2,1)} copy(bf16[16,65536]{1,0:T(8,128)(2,1)} %convert_element_type.30) | data formatting | bytes 4194304 | tf_op jit(solution)/shard_map/convert_element_type | solution.py:59
  462.2 131.7 %gather_fusion = bf16[36864,16]{1,0:T(8,128)(2,1)} fusion(bf16[16,65536]{0,1:T(8,128)(2,1)} %copy.46, s32[36864]{0:T(1024)S(1)} %copy-done.3), kind=kCustom, calls=%fused_computation | custom fusion | bytes 2506752 | tf_op jit(solution)/shard_map/jit(_take)/gather | solution.py:61
  594.0 8.6 %copy.47 = bf16[16,128,288]{2,0,1:T(8,128)(2,1)} copy(bf16[16,128,288]{0,2,1:T(8,128)(2,1)} %bitcast.31) | data formatting | bytes 2359296 | tf_op jit(solution)/shard_map/jit(_take)/gather | solution.py:61
  605.5 11.4 %all-to-all-start = ((bf16[16,128,288]{2,0,1:T(8,128)(2,1)}), bf16[16,128,288]{2,0,1:T(8,128)(2,1)}, u32[]{:S(2)}, u32[]{:S(2)}) async-start(bf16[16,128,288]{2,0,1:T(8,128)(2,1)} %broadcast_select_fusion), calls=%async_computation.1 | async-start | bytes 3145728 | tf_op jit(solution)/shard_map/all_to_all | solution.py:62
  619.7 22.3 %all-to-all-done = bf16[16,128,288]{2,0,1:T(8,128)(2,1)} async-done(((bf16[16,128,288]{2,0,1:T(8,128)(2,1)}), bf16[16,128,288]{2,0,1:T(8,128)(2,1)}, u32[]{:S(2)}, u32[]{:S(2)}) %all-to-all-start) | async-done | bytes 1179680 | tf_op jit(solution)/shard_map/all_to_all | solution.py:62
  646.7 7.6 %broadcast_multiply_fusion = bf16[16,12,36864]{2,1,0:T(8,128)(2,1)} fusion(bf16[12,36864]{1,0:T(8,128)(2,1)S(1)} %fusion.5, bf16[16,36864]{1,0:T(8,128)(2,1)} %mul.19), kind=kLoop, calls=%fused_computation.9 | loop fusion | flops 7077888 | bytes 16220160 | tf_op jit(solution)/shard_map/mul | solution.py:75
  654.3 14.4 %mul.23 = bf16[192,36864]{1,0:T(8,128)(2,1)} reshape(bf16[16,12,36864]{2,1,0:T(8,128)(2,1)} %broadcast_multiply_fusion) | data formatting | bytes 28311552 | tf_op jit(solution)/shard_map/mul | solution.py:75
  668.7 22.3 %fusion.11 = f32[192,128]{1,0:T(8,128)S(1)} fusion(bf16[192,36864]{1,0:T(8,128)(2,1)} %mul.23, s32[36864]{0:T(1024)S(1)} %copy-done.5), kind=kOutput, calls=%fused_computation.24 | convolution fusion | flops 1816682496 | bytes 14401536 | tf_op jit(solution)/shard_map/dot_general | solution.py:76
  (77 shorter events, 111.9 us)
Async XLA Ops:
  7.2 8.4 %copy-start = (bf16[16,512]{1,0:T(8,128)(2,1)S(1)}, bf16[16,512]{1,0:T(8,128)(2,1)}, u32[]{:S(2)}) copy-start(bf16[16,512]{1,0:T(8,128)(2,1)} %param.11) | copy-start | bytes 49156
  7.2 683.9 %reduce-scatter.2.cloned.1.call-start = ((), (), s32[]{:S(2)}) async-start(), calls=%async_computation.2 | async-start | bytes 491520 | tf_op jit(solution)/shard_map/reduce_scatter | solution.py:79
  8.4 13.8 %collective-permute-start = (bf16[16,9,512]{2,0,1:T(8,128)(2,1)S(1)}, bf16[16,9,512]{2,0,1:T(8,128)(2,1)S(1)}, u32[]{:S(2)}, u32[]{:S(2)}) collective-permute-start(bf16[16,9,512]{2,0,1:T(8,128)(2,1)S(1)} %copy.51), channel_id=1, source_target_pairs={{0,4},{4,8},{8,12},{12,16},{16,20},{20,24},{24,28},{28,32},{32,36}... | collective-permute-start | bytes 442376 | tf_op jit(solution)/shard_map/ppermute | solution.py:17
  13.5 6.6 copy-start.2
  13.5 7.3 %copy-start.4 = (s32[36864]{0:T(1024)S(1)}, s32[36864]{0:T(1024)}, u32[]{:S(2)}) copy-start(s32[36864]{0:T(1024)} %param.13) | copy-start | bytes 442372
  13.5 11.6 %collective-permute-start.1 = (bf16[16,9,512]{2,0,1:T(8,128)(2,1)S(1)}, bf16[16,9,512]{2,0,1:T(8,128)(2,1)S(1)}, u32[]{:S(2)}, u32[]{:S(2)}) collective-permute-start(bf16[16,9,512]{2,0,1:T(8,128)(2,1)S(1)} %copy.52), channel_id=1, source_target_pairs={{4,0},{8,4},{12,8},{16,12},{20,16},{24,20},{28,24},{32,28},{36,32}... | collective-permute-start | bytes 442376 | tf_op jit(solution)/shard_map/ppermute | solution.py:19
  25.1 9.7 %copy-start.6 = (bf16[19,19]{1,0:T(8,128)(2,1)S(1)}, bf16[19,19]{1,0:T(8,128)(2,1)}, u32[]{:S(2)}) copy-start(bf16[19,19]{1,0:T(8,128)(2,1)} %param.9) | copy-start | bytes 2170
  28.5 8.7 %collective-permute-start.2 = (bf16[16,146,9]{1,0,2:T(8,128)(2,1)}, bf16[16,146,9]{1,0,2:T(8,128)(2,1)}, u32[]{:S(2)}, u32[]{:S(2)}) collective-permute-start(bf16[16,146,9]{1,0,2:T(8,128)(2,1)} %copy.38), channel_id=1, source_target_pairs={{0,1},{1,2},{2,3},{4,5},{5,6},{6,7},{8,9},{9,10},{10,11},{12,13},{... | collective-permute-start | bytes 126152 | tf_op jit(solution)/shard_map/ppermute | solution.py:17
  33.5 5.7 collective-permute-start.3
  449.8 12.4 %copy-start.3 = (s32[36864]{0:T(1024)S(1)}, s32[36864]{0:T(1024)}, u32[]{:S(2)}) copy-start(s32[36864]{0:T(1024)} %fusion.14) | copy-start | bytes 442372
  605.5 36.5 %all-to-all-start = ((bf16[16,128,288]{2,0,1:T(8,128)(2,1)}), bf16[16,128,288]{2,0,1:T(8,128)(2,1)}, u32[]{:S(2)}, u32[]{:S(2)}) async-start(bf16[16,128,288]{2,0,1:T(8,128)(2,1)} %broadcast_select_fusion), calls=%async_computation.1 | async-start | bytes 3145728 | tf_op jit(solution)/shard_map/all_to_all | solution.py:62
  654.3 14.4 %copy-start.5 = (s32[36864]{0:T(1024)S(1)}, s32[36864]{0:T(1024)}, u32[]{:S(2)}) copy-start(s32[36864]{0:T(1024)} %get-tuple-element.129) | copy-start | bytes 442372
  668.7 23.9 %copy-start.1 = (bf16[16,512]{1,0:T(8,128)(2,1)S(1)}, bf16[16,512]{1,0:T(8,128)(2,1)}, u32[]{:S(2)}) copy-start(bf16[16,512]{1,0:T(8,128)(2,1)} %param.11) | copy-start | bytes 49156
Sparse Core Ops, SparseCore 0:
  20.2 20.6 reduce-scatter.1
where the time goes:
time: 704 us; the launch traced here: 699 us
  local copies, waits for them, and re-layouts  461 us (65%)
  matrix products  154 us (22%)
  starting transfers between devices  23.5 us (3%)
  other arithmetic  23.5 us (3%)
  waiting for transfers between devices  22.7 us (3%)
  between operations  14.3 us (2%)
    reshape x19, local copies, waits for them, and re-layouts, add_offset(): taken.reshape(-1, window)  145 us
    gather x2, local copies, waits for them, and re-layouts, body(): outgoing = jnp.take(flat_tile, send_pix, axis=1)  140 us
    dot_general x19, matrix products, add_offset(): jnp.dot(taken.reshape(-1, window), banded[offset_row], preferred_element_...  127 us
    dynamic_slice x38, local copies, waits for them, and re-layouts, add_offset(): taken = lax.dynamic_slice_in_dim(stacked, offset_row, tile_rows, axis=1)  126 us
    dot_general x1, matrix products, body(): totals = jnp.dot(masked, low_table, preferred_element_type=jnp.float32)  22.3 us
    all_to_all x1, waiting for transfers between devices, body(): lax.all_to_all(outgoing, ('row', 'col'), split_axis=1, concat_axis=1, til...  22.3 us
    mul x2, local copies, waits for them, and re-layouts, body(): incoming[:, None, :] * high_table[None, :, :]  17.3 us
    convert_element_type x3, local copies, waits for them, and re-layouts, body(): running.reshape(band_count, tile_rows, tile_cols).astype(jnp.bfloat16)  16.8 us
  transfers between devices with their start and end apart: 6, of which 2 were waited for; matrix products, arithmetic and copies ran while one was open for 91% of the time, Pallas kernels for 0%

commit v1 on v0

v1 whole, which is shorter than its diff:
```python
import functools

import jax
import jax.numpy as jnp
import numpy as np
from jax import lax
from jax.experimental import pallas as pl
from jax.experimental.pallas import tpu as pltpu
from jax.sharding import PartitionSpec as P

NSAMP = 16
BANDS = 16
KS = 19
TR = 128
TC = 512
FPD = 1536
ND = 128
CAP = 288
N_COL = 4
UNITS = 8
ROWS = CAP // UNITS
PADR = 40
QUART = 4
PERQ = ND // QUART
CELLS = TR // 8 * TC
HI = FPD // 128
MESH = pl.DeviceIdType.MESH


def blur_kernel(p_ref, w_ref, out_ref, tab_ref, s_ref):
    def block(yb, carry):
        acc = None
        for a in range(KS + 1):
            left = jnp.concatenate(
                [
                    p_ref[pl.ds(yb * 8 + a // 2, 8), a % 2, :, j * 128 : j * 128 + 256].reshape(128, 256)
                    for j in range(4)
                ],
                axis=0,
            )
            right = jnp.concatenate([w_ref[a + 1], w_ref[a]], axis=1)
            term = jnp.dot(left, right, preferred_element_type=jnp.float32)
            acc = term if acc is None else acc + term
        rounded = acc.astype(jnp.bfloat16).astype(jnp.float32)
        for j in range(4):
            rows = [
                rounded[j * 128 + m * 16 : j * 128 + m * 16 + 16, q * 128 : q * 128 + 128]
                for m in range(8)
                for q in range(2)
            ]
            for h in range(2):
                piece = jnp.concatenate(rows[8 * h : 8 * h + 8], axis=0)
                s_ref[j, pl.ds(h * 128, 128), :] = piece
                at = pl.multiple_of((2 * yb + h) * TC + j * 128, 128)
                tab_ref[pl.ds(at, 128), :] = jnp.transpose(piece)
            for b in range(BANDS):
                out_ref[b, pl.ds(pl.multiple_of(yb * 16, 16), 16), j * 128 : j * 128 + 128] = s_ref[
                    j, pl.ds(b, 16, stride=16), :
                ].astype(jnp.bfloat16)
        return carry

    lax.fori_loop(0, TR // 16, block, 0)


def collect_kernel(
    idx_ref, tab_ref, foot_ref, out_ref, rot, stage, send, recv, wide, acc, send_sem, recv_sem
):
    me = lax.axis_index("row") * N_COL + lax.axis_index("col")
    mq = me // PERQ
    ml = lax.rem(me, PERQ)

    barrier = pltpu.get_barrier_semaphore()

    def greet(i, carry):
        other = lax.rem(me + i, ND)
        pl.semaphore_signal(
            barrier, inc=1, device_id=(other // N_COL, lax.rem(other, N_COL)), device_id_type=MESH
        )
        return carry

    lax.fori_loop(1, ND, greet, 0)

    def turn(i, carry):
        cells = tab_ref[pl.ds(pl.multiple_of(i * 128, 128), 128), :]
        for j in range(UNITS):
            at = pl.multiple_of(j * CELLS + i * 128, 128)
            rot[pl.ds(at, 128), :] = pltpu.roll(cells, 16 * j, 1) if j else cells
        return carry

    lax.fori_loop(0, CELLS // 128, turn, 0)
    stage[...] = jnp.zeros(stage.shape, jnp.float32)
    acc[...] = jnp.zeros(acc.shape, jnp.float32)

    def gather(dest):
        base = dest * CAP
        for k in range(CAP):
            u, r = k // ROWS, k % ROWS
            lanes = slice(16 * u, 16 * u + 16)
            stage[r : r + 1, lanes] = rot[pl.ds(idx_ref[base + k], 1), lanes]
        return stage[...].astype(jnp.bfloat16)

    recv[me] = gather(me)
    pl.semaphore_wait(barrier, ND - 1)

    def push(n, carry):
        t = n // PERQ
        i = lax.rem(n, PERQ)
        dest = lax.rem(mq + t, QUART) * PERQ + lax.rem(ml + i, PERQ)
        send[dest] = gather(dest)
        pltpu.make_async_remote_copy(
            src_ref=send.at[dest],
            dst_ref=recv.at[me],
            send_sem=send_sem,
            recv_sem=recv_sem.at[t],
            device_id=(dest // N_COL, lax.rem(dest, N_COL)),
            device_id_type=MESH,
        ).start()
        return carry

    lax.fori_loop(1, ND, push, 0)

    def add_up(t):
        first = lax.rem(mq - t + QUART, QUART) * PERQ
        for g in range(PERQ):
            at = pl.multiple_of((first + g) * PADR, 8)
            wide[pl.ds(at, PADR), :] = recv[first + g].astype(jnp.float32)

        def chunk(c, carry):
            at = pl.multiple_of(first * PADR + c * 128, 128)
            cols = jnp.transpose(wide[pl.ds(at, 128), :])
            masked, low = [], []
            for u in range(UNITS):
                foot = foot_ref[pl.ds(u, 1), pl.ds(at, 128)]
                hi = jnp.broadcast_to(lax.shift_right_logical(foot, 7), (BANDS, 128))
                lo = jnp.broadcast_to(foot & 127, (128, 128))
                vals = cols[16 * u : 16 * u + 16]
                masked.append(
                    jnp.concatenate([jnp.where(hi == h, vals, 0.0) for h in range(HI)], axis=0).astype(
                        jnp.bfloat16
                    )
                )
                hit = lo == lax.broadcasted_iota(jnp.int32, (128, 128), 0)
                low.append(jnp.where(hit, 1.0, 0.0).astype(jnp.bfloat16))
            acc[...] += lax.dot_general(
                jnp.concatenate(masked, axis=1),
                jnp.concatenate(low, axis=1),
                (((1,), (1,)), ((), ())),
                preferred_element_type=jnp.float32,
            )
            return carry

        lax.fori_loop(0, PERQ * PADR // 128, chunk, 0)

    for t in range(QUART):
        count = PERQ - 1 if t == 0 else PERQ
        pltpu.make_async_copy(send.at[pl.ds(0, count)], recv.at[pl.ds(0, count)], recv_sem.at[t]).wait()
        add_up(t)
    for h in range(HI):
        out_ref[:, 128 * h : 128 * h + 128] = acc[16 * h : 16 * h + 16, :] * (1.0 / NSAMP)
    pltpu.make_async_copy(send.at[pl.ds(0, ND - 1)], recv.at[pl.ds(0, ND - 1)], send_sem).wait()


def with_halo(cells, axis, dim, width):
    count = lax.axis_size(axis)
    head = lax.slice_in_dim(cells, 0, width, axis=dim)
    tail = lax.slice_in_dim(cells, cells.shape[dim] - width, cells.shape[dim], axis=dim)
    before = lax.ppermute(tail, axis, [(i, i + 1) for i in range(count - 1)])
    after = lax.ppermute(head, axis, [(i + 1, i) for i in range(count - 1)])
    return before, cells, after


def body(disk, response, spectra, srf, send_pix, recv_foot):
    margin = KS // 2
    vmem = pl.BlockSpec(memory_space=pltpu.VMEM)

    shifts = np.arange(256)[:, None] - np.arange(128)[None, :]
    picker = jnp.asarray(
        (shifts[None] == np.arange(KS)[:, None, None]).reshape(KS, -1), dtype=jnp.bfloat16
    )
    taps = jnp.pad(response, ((1, 1), (0, 0)))
    bands = jnp.dot(taps, picker, preferred_element_type=jnp.float32).astype(jnp.bfloat16)
    bands = bands.reshape(KS + 2, 256, 128)

    turned = jnp.transpose(disk, (1, 0, 2))
    rows = jnp.concatenate(with_halo(turned, "row", 0, margin), axis=0)
    cols = jnp.concatenate(with_halo(rows, "col", 2, margin), axis=2)
    padded = jnp.pad(cols, ((0, 2), (0, 0), (0, 640 - TC - 2 * margin)))
    padded = padded.reshape(74, 2, BANDS, 640)

    blurred, table = pl.pallas_call(
        blur_kernel,
        out_shape=(
            jax.ShapeDtypeStruct((BANDS, TR, TC), jnp.bfloat16),
            jax.ShapeDtypeStruct((CELLS, 128), jnp.float32),
        ),
        in_specs=[vmem, vmem],
        out_specs=(vmem, vmem),
        scratch_shapes=[pltpu.VMEM((4, 256, 128), jnp.float32)],
        compiler_params=pltpu.CompilerParams(vmem_limit_bytes=40 << 20),
        cost_estimate=pl.CostEstimate(flops=10 << 30, bytes_accessed=10 << 20, transcendentals=0),
        name="blur",
    )(padded, bands)

    slot = lax.rem(lax.iota(jnp.int32, ND * CAP), jnp.int32(CAP)) // ROWS
    cell = ((send_pix >> 12) << 9) | (send_pix & 511)
    idx = (((slot - (send_pix >> 9)) & 7) << 13) | cell

    foot = recv_foot.reshape(ND, UNITS, ROWS)
    foot = jnp.pad(foot, ((0, 0), (0, 0), (0, PADR - ROWS)), constant_values=FPD)
    foot = jnp.transpose(foot, (1, 0, 2)).reshape(UNITS, ND * PADR)

    partial_bands = jnp.dot(srf, spectra, preferred_element_type=jnp.float32)
    evolved = lax.psum_scatter(partial_bands, "col", scatter_dimension=1, tiled=True)

    imager = pl.pallas_call(
        collect_kernel,
        out_shape=jax.ShapeDtypeStruct((BANDS, FPD), jnp.float32),
        in_specs=[pl.BlockSpec(memory_space=pltpu.SMEM), vmem, vmem],
        out_specs=vmem,
        scratch_shapes=[
            pltpu.VMEM((UNITS * CELLS, 128), jnp.float32),
            pltpu.VMEM((PADR, 128), jnp.float32),
            pltpu.VMEM((ND, PADR, 128), jnp.bfloat16),
            pltpu.VMEM((ND, PADR, 128), jnp.bfloat16),
            pltpu.VMEM((ND * PADR, 128), jnp.float32),
            pltpu.VMEM((HI * BANDS, 128), jnp.float32),
            pltpu.SemaphoreType.DMA,
            pltpu.SemaphoreType.DMA((QUART,)),
        ],
        compiler_params=pltpu.CompilerParams(
            vmem_limit_bytes=52 << 20, collective_id=0, has_side_effects=True
        ),
        cost_estimate=pl.CostEstimate(flops=4 << 30, bytes_accessed=10 << 20, transcendentals=0),
        name="collect",
    )(idx, table, foot)
    return (blurred, evolved - imager)


def solution(mesh):
    placed = (
        P(None, "row", "col"),
        P(),
        P("col", "row"),
        P(None, "col"),
        P(("row", "col")),
        P(("row", "col")),
    )
    return jax.shard_map(
        body,
        mesh=mesh,
        in_specs=placed,
        out_specs=(P(None, "row", "col"), P(None, ("row", "col"))),
        check_vma=False,
    )
```

time: 704 us -> 135 us (0.19)
  local copies, waits for them, and re-layouts: 461 us -> 13.6 us
  matrix products: 154 us -> 7.66 us
  Pallas kernels: 0 us -> 78.2 us
  waiting for transfers between devices: 22.7 us -> 0.88 us
  other arithmetic: 23.5 us -> 6.83 us
  starting transfers between devices: 23.5 us -> 11.4 us
    dot_general x21 -> x1, matrix products: 150 us -> 3.17 us  [body(): jnp.dot(taps, picker, preferred_element_type=jnp.float32)]
    reshape x19 -> x3, local copies, waits for them, and re-layouts: 145 us -> 1.85 us  [the longest x1 1.43 us: body(): foot = recv_foot.reshape(ND, UNITS, ROWS)]
    gather x2 -> x0, local copies, waits for them, and re-layouts: 140 us -> none  [body(): outgoing = jnp.take(flat_tile, send_pix, axis=1)]
    dynamic_slice x38 -> x0, local copies, waits for them, and re-layouts: 126 us -> none  [add_offset(): taken = lax.dynamic_slice_in_dim(stacked, offset_row, tile_rows, axis=1)]
    pallas_call x0 -> x2, Pallas kernels: none -> 78.2 us  [the longest x1 63.4 us: body(): pl.pallas_call(collect_kernel, out_shape=jax.ShapeDtypeStruct((BANDS, FPD...]
    all_to_all x1 -> x0, waiting for transfers between devices: 22.3 us -> none  [body(): lax.all_to_all(outgoing, ('row', 'col'), split_axis=1, concat_axis=1, til...]
    mul x2 -> x0, local copies, waits for them, and re-layouts: 17.3 us -> none  [body(): incoming[:, None, :] * high_table[None, :, :]]
    convert_element_type x3 -> x0, local copies, waits for them, and re-layouts: 16.8 us -> none  [body(): running.reshape(band_count, tile_rows, tile_cols).astype(jnp.bfloat16)]
  transfers between devices with their start and end apart: 6 -> 5, of which waited for: 2 -> 1; matrix products, arithmetic and copies ran while one was open for 91% -> 16% of each run, Pallas kernels for 0% -> 59%
where the time goes in v1:
time: 135 us; the launch traced here: 133 us
  Pallas kernels  78.2 us (58%)
  between operations  14.2 us (11%)
  local copies, waits for them, and re-layouts  13.6 us (10%)
  starting transfers between devices  11.4 us (8%)
  matrix products  7.66 us (6%)
  other arithmetic  6.83 us (5%)
    pallas_call x1, Pallas kernels, body(): pl.pallas_call(collect_kernel, out_shape=jax.ShapeDtypeStruct((BANDS, FPD...  63.4 us
    pallas_call x1, Pallas kernels, body(): pl.pallas_call(blur_kernel, out_shape=(jax.ShapeDtypeStruct((BANDS, TR, T...  14.9 us
    ppermute x2, starting transfers between devices, with_halo(): before = lax.ppermute(tail, axis, [(i, i + 1) for i in range(count - 1)])  8.05 us
    unnamed x16, local copies, waits for them, and re-layouts  7.15 us
    dot_general x1, matrix products, body(): partial_bands = jnp.dot(srf, spectra, preferred_element_type=jnp.float32)  4.49 us
    concatenate x1, other arithmetic, body(): cols = jnp.concatenate(with_halo(rows, 'col', 2, margin), axis=2)  4 us
    ppermute x2, starting transfers between devices, with_halo(): after = lax.ppermute(head, axis, [(i + 1, i) for i in range(count - 1)])  3.34 us
    dot_general x1, matrix products, body(): jnp.dot(taps, picker, preferred_element_type=jnp.float32)  3.17 us
  transfers between devices with their start and end apart: 5, of which 1 were waited for; matrix products, arithmetic and copies ran while one was open for 16% of the time, Pallas kernels for 59%

profile of v1, /device:TPU:1, one launch (start us, length us, event | category | flops | bytes accessed | tf_op | source)
XLA Modules:
  0.0 132.9 jit_solution(2617646681503262355)
XLA Ops:
  7.2 0.0 copy-start
  7.2 0.0 reduce-scatter.2.cloned.1.call-start
  7.2 2.8 %copy.23 = bf16[16,128,512]{2,0,1:T(8,128)(2,1)S(1)} copy(bf16[16,128,512]{2,1,0:T(8,128)(2,1)} %param.7) | data formatting | bytes 4194304 | tf_op args[0]
  10.0 0.0 copy-start.2
  10.0 4.9 %collective-permute-start = (bf16[9,16,512]{2,1,0:T(8,128)(2,1)S(1)}, bf16[9,16,512]{2,1,0:T(8,128)(2,1)S(1)}, u32[]{:S(2)}, u32[]{:S(2)}) collective-permute-start(bf16[9,16,512]{2,1,0:T(8,128)(2,1)S(1)} %get-tuple-element.8), channel_id=1, source_target_pairs={{0,4},{4,8},{8,12},{12,16},{16,20},{20,24},{24,28},{28,32},{32,36}... | collective-permute-start | bytes 442376 | tf_op jit(solution)/shard_map/ppermute | solution.py:167
  15.0 0.0 copy-start.4
  15.0 0.0 copy-start.6
  15.0 2.1 %collective-permute-start.1 = (bf16[9,16,512]{2,1,0:T(8,128)(2,1)S(1)}, bf16[9,16,512]{2,1,0:T(8,128)(2,1)}, u32[]{:S(2)}, u32[]{:S(2)}) collective-permute-start(bf16[9,16,512]{2,1,0:T(8,128)(2,1)S(1)} %get-tuple-element.9), channel_id=1, source_target_pairs={{4,0},{8,4},{12,8},{16,12},{20,16},{24,20},{28,24},{32,28},{36,32}... | collective-permute-start | bytes 442376 | tf_op jit(solution)/shard_map/ppermute | solution.py:168
  17.1 0.0 copy-done
  17.1 4.5 %fusion.23 = f32[16,6144]{1,0:T(8,128)} fusion(bf16[16,512]{1,0:T(8,128)(2,1)S(1)} %copy-done, bf16[512,6144]{1,0:T(8,128)(2,1)} %param.9), kind=kOutput, calls=%fused_computation.35 | convolution fusion | flops 100663296 | bytes 6701056 | tf_op jit(solution)/shard_map/dot_general | solution.py:212
  21.5 0.0 copy-start.5
  21.5 0.0 reduce-scatter.2.cloned.1.call-update
  21.6 0.0 copy-done.4
  21.6 0.2 fusion.18.idx_ref
  21.8 0.0 copy-done.6
  21.8 3.2 %convolution_convert_fusion = bf16[21,32768]{1,0:T(8,128)(2,1)} fusion(bf16[19,32768]{1,0:T(8,128)(2,1)} %constant.30.clone, bf16[19,19]{1,0:T(8,128)(2,1)S(1)} %copy-done.6), kind=kOutput, calls=%fused_computation | convolution fusion | flops 26836992 | bytes 2622162 | tf_op jit(solution)/shard_map/dot_general | solution.py:181
  24.9 0.0 copy-done.5
  24.9 1.4 %reshape.18 = s32[128,8,36]{2,1,0:T(8,128)} reshape(s32[36864]{0:T(1024)S(1)} %copy-done.5) | data formatting | bytes 294912 | tf_op jit(solution)/shard_map/reshape | solution.py:208
  26.4 0.0 collective-permute-done
  26.4 0.0 copy-start.3
  26.4 0.7 copy-done.3
  27.1 0.0 collective-permute-done.1
  27.1 1.1 pad_maximum_fusion.2
  28.2 0.6 copy.16
  28.8 3.1 %collective-permute-start.2 = (bf16[146,16,9]{0,1,2:T(8,128)(2,1)S(1)}, bf16[146,16,9]{0,1,2:T(8,128)(2,1)S(1)}, u32[]{:S(2)}, u32[]{:S(2)}) collective-permute-start(bf16[146,16,9]{0,1,2:T(8,128)(2,1)S(1)} %copy.16), channel_id=1, source_target_pairs={{0,1},{1,2},{2,3},{4,5},{5,6},{6,7},{8,9},{9,10},{10,11},{12,13},{... | collective-permute-start | bytes 126152 | tf_op jit(solution)/shard_map/ppermute | solution.py:167
  31.9 0.6 copy.17
  32.5 1.3 collective-permute-start.3
  33.8 1.1 pad_bitcast_fusion
  34.9 1.7 %copy.21 = bf16[3,8,256,128]{3,2,1,0:T(8,128)(2,1)S(1)} copy(bf16[3,8,256,128]{3,1,2,0:T(8,128)(2,1)} %bitcast.16) | data formatting | bytes 3145728
  36.7 0.0 copy-done.2
  36.7 0.1 slice.18.w_ref
  36.8 0.1 copy.20
  36.9 0.3 reshape.19.foot_ref
  37.2 0.0 collective-permute-done.2
  37.2 0.7 copy.18
  37.9 0.8 collective-permute-done.3
  38.7 1.5 %copy.19 = bf16[146,16,9]{2,1,0:T(8,128)(2,1)S(1)} copy(bf16[146,16,9]{0,1,2:T(8,128)(2,1)} %collective-permute-done.3) | data formatting | bytes 84096 | tf_op jit(solution)/shard_map/ppermute | solution.py:168
  40.3 4.0 %fusion.8 = bf16[148,16,640]{2,1,0:T(8,128)(2,1)S(1)} fusion(bf16[146,16,9]{2,1,0:T(8,128)(2,1)S(1)} %copy.19, bf16[146,16,9]{2,1,0:T(8,128)(2,1)S(1)} %copy.18, bf16[9,16,512]{2,1,0:T(8,128)(2,1)} %collective-permute-done.1, bf16[128,16,512]{2,1,0:T(8,128)(2,1)} %bitcast.15, bf16[9,16,512]{2,1,0:T(8,128)(2,1)} %copy-done.3), kind=kLoop, calls=%fused_computation.11 | loop fusion | flops 34856960 | bytes 5507200 | tf_op jit(solution)/shard_map/concatenate | solution.py:186
  44.3 14.9 %blur.1 = (bf16[16,128,512]{2,1,0:T(8,128)(2,1)}, f32[8192,128]{1,0:T(8,128)S(1)}) custom-call(bf16[74,2,16,640]{3,2,1,0:T(8,128)(2,1)S(1)} %bitcast.12, bf16[21,256,128]{2,1,0:T(8,128)(2,1)S(1)} %slice.18.w_ref), custom_call_target="tpu_custom_call" | custom-call | flops 10737418240 | bytes 10485760 | tf_op jit(solution)/shard_map/blur/pallas_call | solution.py:190
  59.1 0.0 copy-start.1
  59.1 1.9 %copy-done.1 = f32[8192,128]{1,0:T(8,128)} copy-done((f32[8192,128]{1,0:T(8,128)}, f32[8192,128]{1,0:T(8,128)S(1)}, u32[]{:S(2)}) %copy-start.1) | copy-done | bytes 4194328
  61.1 63.4 %collect.1 = f32[16,1536]{1,0:T(8,128)S(1)} custom-call(s32[36864]{0:T(1024)S(1)} %fusion.18.idx_ref, f32[8192,128]{1,0:T(8,128)} %copy-done.1, s32[8,5120]{1,0:T(8,128)S(1)} %reshape.19.foot_ref), custom_call_target="tpu_custom_call" | custom-call | flops 4294967296 | bytes 10485760 | tf_op jit(solution)/shard_map/collect/pallas_call | solution.py:215
  124.4 0.0 reduce-scatter.2.cloned.1.call-done
  124.5 1.5 %sub.14 = f32[16,1536]{1,0:T(8,128)} subtract(f32[16,1536]{1,0:T(8,128)} %reduce-scatter.2.cloned.1.call-done, f32[16,1536]{1,0:T(8,128)S(1)} %collect.1) | non-fusion elementwise | flops 24576 | bytes 294912 | tf_op jit(solution)/shard_map/sub | solution.py:236
  (1 shorter events, 0.0 us)
Async XLA Ops:
  7.2 9.9 %copy-start = (bf16[16,512]{1,0:T(8,128)(2,1)S(1)}, bf16[16,512]{1,0:T(8,128)(2,1)}, u32[]{:S(2)}) copy-start(bf16[16,512]{1,0:T(8,128)(2,1)} %param.10) | copy-start | bytes 49156
  7.2 117.3 %reduce-scatter.2.cloned.1.call-start = ((), (), s32[]{:S(2)}) async-start(), calls=%async_computation.1 | async-start | bytes 491520 | tf_op jit(solution)/shard_map/reduce_scatter | solution.py:213
  10.0 26.7 %copy-start.2 = (bf16[16,128,512]{2,0,1:T(8,128)(2,1)}, bf16[16,128,512]{2,0,1:T(8,128)(2,1)S(1)}, u32[]{:S(2)}) copy-start(bf16[16,128,512]{2,0,1:T(8,128)(2,1)S(1)} %copy.23) | copy-start | bytes 6291460
  10.0 16.4 %collective-permute-start = (bf16[9,16,512]{2,1,0:T(8,128)(2,1)S(1)}, bf16[9,16,512]{2,1,0:T(8,128)(2,1)S(1)}, u32[]{:S(2)}, u32[]{:S(2)}) collective-permute-start(bf16[9,16,512]{2,1,0:T(8,128)(2,1)S(1)} %get-tuple-element.8), channel_id=1, source_target_pairs={{0,4},{4,8},{8,12},{12,16},{16,20},{20,24},{24,28},{28,32},{32,36}... | collective-permute-start | bytes 442376 | tf_op jit(solution)/shard_map/ppermute | solution.py:167
  15.0 6.6 %copy-start.4 = (s32[36864]{0:T(1024)S(1)}, s32[36864]{0:T(1024)}, u32[]{:S(2)}) copy-start(s32[36864]{0:T(1024)} %param.11) | copy-start | bytes 442372
  15.0 6.8 %copy-start.6 = (bf16[19,19]{1,0:T(8,128)(2,1)S(1)}, bf16[19,19]{1,0:T(8,128)(2,1)}, u32[]{:S(2)}) copy-start(bf16[19,19]{1,0:T(8,128)(2,1)} %param.8) | copy-start | bytes 2170
  15.0 12.1 %collective-permute-start.1 = (bf16[9,16,512]{2,1,0:T(8,128)(2,1)S(1)}, bf16[9,16,512]{2,1,0:T(8,128)(2,1)}, u32[]{:S(2)}, u32[]{:S(2)}) collective-permute-start(bf16[9,16,512]{2,1,0:T(8,128)(2,1)S(1)} %get-tuple-element.9), channel_id=1, source_target_pairs={{4,0},{8,4},{12,8},{16,12},{20,16},{24,20},{28,24},{32,28},{36,32}... | collective-permute-start | bytes 442376 | tf_op jit(solution)/shard_map/ppermute | solution.py:168
  21.5 3.4 %copy-start.5 = (s32[36864]{0:T(1024)S(1)}, s32[36864]{0:T(1024)}, u32[]{:S(2)}) copy-start(s32[36864]{0:T(1024)} %param.12) | copy-start | bytes 442372
  26.4 0.7 copy-start.3
  28.8 8.4 %collective-permute-start.2 = (bf16[146,16,9]{0,1,2:T(8,128)(2,1)S(1)}, bf16[146,16,9]{0,1,2:T(8,128)(2,1)S(1)}, u32[]{:S(2)}, u32[]{:S(2)}) collective-permute-start(bf16[146,16,9]{0,1,2:T(8,128)(2,1)S(1)} %copy.16), channel_id=1, source_target_pairs={{0,1},{1,2},{2,3},{4,5},{5,6},{6,7},{8,9},{9,10},{10,11},{12,13},{... | collective-permute-start | bytes 126152 | tf_op jit(solution)/shard_map/ppermute | solution.py:167
  32.5 6.2 %collective-permute-start.3 = (bf16[146,16,9]{0,1,2:T(8,128)(2,1)S(1)}, bf16[146,16,9]{0,1,2:T(8,128)(2,1)}, u32[]{:S(2)}, u32[]{:S(2)}) collective-permute-start(bf16[146,16,9]{0,1,2:T(8,128)(2,1)S(1)} %copy.17), channel_id=1, source_target_pairs={{1,0},{2,1},{3,2},{5,4},{6,5},{7,6},{9,8},{10,9},{11,10},{13,12},{... | collective-permute-start | bytes 126152 | tf_op jit(solution)/shard_map/ppermute | solution.py:168
  59.1 1.9 %copy-start.1 = (f32[8192,128]{1,0:T(8,128)}, f32[8192,128]{1,0:T(8,128)S(1)}, u32[]{:S(2)}) copy-start(f32[8192,128]{1,0:T(8,128)S(1)} %get-tuple-element.5.tab_ref) | copy-start | bytes 12582916
Sparse Core Ops, SparseCore 0:
  21.7 20.6 reduce-scatter.1

commit v2 on v0

v2 whole, which is shorter than its diff:
```python
import jax
import jax.numpy as jnp
from jax import lax
from jax.experimental import pallas as pl
from jax.experimental.pallas import tpu as pltpu
from jax.sharding import PartitionSpec as P

NSAMP = 16
BANDS = 16
KS = 19
EDGE = KS // 2
TR = 128
TC = 512
FPD = 1536
ND = 128
N_ROW = 32
N_COL = 4
CAP = 288
UNITS = 8
ROWS = CAP // UNITS
PADR = 40
CELLS = TR // 8 * TC
HI = FPD // 128
SLOTS = 6
TRIPS = 21
LAG = 8
MESH = pl.DeviceIdType.MESH
F32 = jnp.float32
BF16 = jnp.bfloat16


def kernel(
    turned, taps, srf_ref, spectra, idx_ref, foot_ref, blur_out, miss_out,
    own, p_ref, w_ref, spec, part, gains, edge, hrow, hcol, hcor, accb, s_ref, rot, stage, send, recv,
    acc, sm, own_sem, spec_sem, idx_sem, edge_send, edge_recv, part_send, part_recv, send_sem, recv_sem,
):
    row = lax.axis_index("row")
    col = lax.axis_index("col")
    me = row * N_COL + col

    def place(d):
        return (d // N_COL, lax.rem(d, N_COL))

    own_copy = pltpu.make_async_copy(turned, own, own_sem)
    own_copy.start()
    spec_copies = []
    for k in (1, 2, 3, 0):
        at = pl.multiple_of(lax.rem(col + k, N_COL) * FPD, 128)
        copy = pltpu.make_async_copy(spectra.at[:, pl.ds(at, FPD)], spec.at[k], spec_sem.at[k])
        copy.start()
        spec_copies.append((k, copy))

    def step_of(q):
        return q - 1

    def fetch(n, g):
        return pltpu.make_async_copy(idx_ref.at[lax.rem(me + n, ND)], sm.at[g], idx_sem.at[g])

    for g in range(SLOTS):
        fetch((0, ND - 1)[g] if g < 2 else step_of(g), g).start()

    barrier = pltpu.get_barrier_semaphore()

    def greet(i, carry):
        pl.semaphore_signal(barrier, inc=1, device_id=place(lax.rem(me + i, ND)), device_id_type=MESH)
        return carry

    lax.fori_loop(1, ND, greet, 0)

    lane = lax.broadcasted_iota(jnp.int32, (BANDS, 128), 1)
    own_copy.wait()

    def pack(g, carry):
        left = jnp.zeros((BANDS, 128), F32)
        right = jnp.zeros((BANDS, 128), F32)
        for k in range(8):
            a = own[8 * g + k, :, 0:128].astype(F32)
            b = own[8 * g + k, :, TC - 128 : TC].astype(F32)
            left = jnp.where(lane // 16 == k, pltpu.roll(a, 16 * k, 1) if k else a, left)
            right = jnp.where(lane // 16 == k, pltpu.roll(b, (16 * k + EDGE) % 128, 1), right)
        edge[0, g] = left.astype(BF16)
        edge[1, g] = right.astype(BF16)
        return carry

    lax.fori_loop(0, TR // 8, pack, 0)
    pl.semaphore_wait(barrier, ND - 1)

    up, down = lax.rem(row + N_ROW - 1, N_ROW), lax.rem(row + 1, N_ROW)
    west, east = lax.rem(col + N_COL - 1, N_COL), lax.rem(col + 1, N_COL)
    moves = [
        (own.at[pl.ds(0, EDGE)], hrow.at[1], (up, col)),
        (own.at[pl.ds(TR - EDGE, EDGE)], hrow.at[0], (down, col)),
        (edge.at[0], hcol.at[1], (row, west)),
        (edge.at[1], hcol.at[0], (row, east)),
        (edge.at[0, pl.ds(0, 2)], hcor.at[3], (up, west)),
        (edge.at[1, pl.ds(0, 2)], hcor.at[2], (up, east)),
        (edge.at[0, pl.ds(14, 2)], hcor.at[1], (down, west)),
        (edge.at[1, pl.ds(14, 2)], hcor.at[0], (down, east)),
    ]
    edge_copies = [
        pltpu.make_async_remote_copy(
            src_ref=src, dst_ref=dst, send_sem=edge_send.at[i], recv_sem=edge_recv.at[i],
            device_id=there, device_id_type=MESH,
        )
        for i, (src, dst, there) in enumerate(moves)
    ]
    for copy in edge_copies:
        copy.start()

    part_copies = []
    for k, copy in spec_copies:
        copy.wait()
        part[k] = jnp.dot(srf_ref[...], spec[k], preferred_element_type=F32)
        if k:
            out = pltpu.make_async_remote_copy(
                src_ref=part.at[k], dst_ref=gains.at[k], send_sem=part_send.at[k], recv_sem=part_recv.at[k],
                device_id=(row, lax.rem(col + k, N_COL)), device_id_type=MESH,
            )
            out.start()
            part_copies.append(out)

    w_ref[0] = jnp.zeros((256, 128), BF16)
    w_ref[KS + 1] = jnp.zeros((256, 128), BF16)

    def band(a, carry):
        line = jnp.broadcast_to(taps[pl.ds(a, 1), :], (256, 256))
        w_ref[a + 1] = pltpu.roll(line, 0, 1, stride=1, stride_axis=0)[:, :128].astype(BF16)
        return carry

    lax.fori_loop(0, KS, band, 0)

    blank = jnp.zeros((BANDS, 128), F32)

    def shifted(cells):
        return pltpu.roll(jnp.concatenate([cells.astype(F32), blank], axis=1), EDGE, 1)

    def lay(g, carry):
        for k in range(8):
            y = k + EDGE
            p_ref[4 * g + y // 2, y % 2] = shifted(own[8 * g + k]).astype(BF16)
        return carry

    lax.fori_loop(0, TR // 8, lay, 0)
    p_ref[73, 0] = jnp.zeros((BANDS, 640), BF16)
    p_ref[73, 1] = jnp.zeros((BANDS, 640), BF16)

    for copy in edge_copies:
        copy.wait_recv()

    has_up, has_down = row > 0, row < N_ROW - 1
    has_west, has_east = col > 0, col < N_COL - 1

    def west_side(packed, k, tile, keep):
        piece = packed.astype(F32)
        piece = pltpu.roll(piece, 128 - 16 * k, 1) if k else piece
        return jnp.where(lane < EDGE, jnp.where(keep, piece, 0.0), tile)

    def east_side(packed, k, tile, keep):
        piece = pltpu.roll(packed.astype(F32), (128 + EDGE - 16 * k) % 128, 1)
        return jnp.where((lane >= EDGE) & (lane < 2 * EDGE), jnp.where(keep, piece, 0.0), tile)

    def sides(g, carry):
        for k in range(8):
            y = k + EDGE
            at = (4 * g + y // 2, y % 2)
            p_ref[at[0], at[1], :, 0:128] = west_side(
                hcol[0, g], k, p_ref[at[0], at[1], :, 0:128].astype(F32), has_west
            ).astype(BF16)
            p_ref[at[0], at[1], :, TC : TC + 128] = east_side(
                hcol[1, g], k, p_ref[at[0], at[1], :, TC : TC + 128].astype(F32), has_east
            ).astype(BF16)
        return carry

    lax.fori_loop(0, TR // 8, sides, 0)
    for half, first, keep in ((0, 8 - 1, has_up), (1, 0, has_down)):
        for i in range(EDGE):
            y = i if half == 0 else TR + EDGE + i
            g, k = (first + i) // 8, (first + i) % 8
            line = shifted(jnp.where(keep, hrow[half, i].astype(F32), 0.0))
            west_tile = west_side(hcor[2 * half, g], k, line[:, :128], keep & has_west)
            east_tile = east_side(hcor[2 * half + 1, g], k, line[:, TC:], keep & has_east)
            whole = jnp.concatenate([west_tile, line[:, 128:TC], east_tile], axis=1)
            p_ref[y // 2, y % 2] = whole.astype(BF16)

    def products(yb):
        total = None
        for a in range(KS + 1):
            left = jnp.concatenate(
                [
                    p_ref[pl.ds(yb * 8 + a // 2, 8), a % 2, :, j * 128 : j * 128 + 256].reshape(128, 256)
                    for j in range(4)
                ],
                axis=0,
            )
            right = jnp.concatenate([w_ref[a + 1], w_ref[a]], axis=1)
            term = jnp.dot(left, right, preferred_element_type=F32)
            total = term if total is None else total + term
        return total

    def settle(yb):
        rounded = accb[...].astype(BF16).astype(F32)
        for j in range(4):
            lines = [
                rounded[j * 128 + m * 16 : j * 128 + m * 16 + 16, q * 128 : q * 128 + 128]
                for m in range(8)
                for q in range(2)
            ]
            for h in range(2):
                piece = jnp.concatenate(lines[8 * h : 8 * h + 8], axis=0)
                s_ref[j, pl.ds(h * 128, 128), :] = piece
                cells = jnp.transpose(piece)
                for t in range(UNITS):
                    at = pl.multiple_of(t * CELLS + (2 * yb + h) * TC + j * 128, 128)
                    rot[pl.ds(at, 128), :] = pltpu.roll(cells, 16 * t, 1) if t else cells
            for b in range(BANDS):
                blur_out[b, pl.ds(pl.multiple_of(yb * 16, 16), 16), j * 128 : j * 128 + 128] = s_ref[
                    j, pl.ds(b, 16, stride=16), :
                ].astype(BF16)

    accb[...] = products(0)

    def block(yb, carry):
        settle(yb - 1)
        accb[...] = products(yb)
        return carry

    lax.fori_loop(1, TR // 16, block, 0)
    settle(TR // 16 - 1)

    stage[...] = jnp.zeros(stage.shape, F32)
    acc[...] = jnp.zeros(acc.shape, F32)
    lane8 = lax.broadcasted_iota(jnp.int32, (UNITS, 128), 1)

    def gather(g):
        for k in range(CAP):
            u, r = k // ROWS, k % ROWS
            lanes = slice(16 * u, 16 * u + 16)
            stage[g, r : r + 1, lanes] = rot[pl.ds(sm[g, 0, k], 1), lanes]
        return stage[g].astype(BF16)

    def message(n, mark):
        return pltpu.make_async_remote_copy(
            src_ref=send.at[n], dst_ref=recv.at[n], send_sem=send_sem, recv_sem=recv_sem.at[mark],
            device_id=place(lax.rem(me + n, ND)), device_id_type=MESH,
        )

    def arrived(n, count, mark):
        pltpu.make_async_copy(send.at[pl.ds(n, count)], recv.at[pl.ds(n, count)], recv_sem.at[mark]).wait()

    def add_up(steps):
        blocks = [recv[n].astype(F32) for n in steps]
        blocks.append(jnp.zeros((128 - PADR * len(steps), 128), F32))
        foot = jnp.full((UNITS, 128), FPD, jnp.int32)
        for g, n in enumerate(steps):
            feet = foot_ref[lax.rem(me + ND - n, ND)]
            inside = (lane8 >= PADR * g) & (lane8 < PADR * g + PADR)
            foot = jnp.where(inside, pltpu.roll(feet, PADR * g, 1) if g else feet, foot)
        cols = jnp.transpose(jnp.concatenate(blocks, axis=0))
        masked, low = [], []
        for u in range(UNITS):
            hi = jnp.broadcast_to(lax.shift_right_logical(foot[u : u + 1], 7), (BANDS, 128))
            lo = jnp.broadcast_to(foot[u : u + 1] & 127, (128, 128))
            vals = cols[16 * u : 16 * u + 16]
            masked.append(
                jnp.concatenate([jnp.where(hi == h, vals, 0.0) for h in range(HI)], axis=0).astype(BF16)
            )
            hit = lo == lax.broadcasted_iota(jnp.int32, (128, 128), 0)
            low.append(jnp.where(hit, 1.0, 0.0).astype(BF16))
        acc[...] += lax.dot_general(
            jnp.concatenate(masked, axis=1),
            jnp.concatenate(low, axis=1),
            (((1,), (1,)), ((), ())),
            preferred_element_type=F32,
        )

    for g, n in ((0, 0), (1, ND - 1)):
        fetch(n, g).wait()
        if n:
            send[n] = gather(g)
            message(n, 2 * TRIPS).start()
        else:
            recv[0] = gather(g)
        fetch(step_of(g + SLOTS), g).start()

    def half(n, groups, trio, summing):
        for k, g in enumerate(groups):
            fetch(n + k, g).wait()
        if summing:
            back = n - 3 * LAG
            arrived(back, 3, trio - LAG)
            add_up([back, back + 1, back + 2])
        for k, g in enumerate(groups):
            send[n + k] = gather(g)
        for k, g in enumerate(groups):
            message(n + k, trio).start()
            fetch(jnp.minimum(n + k + SLOTS, ND - 1), g).start()

    def turns(summing):
        def turn(i, carry):
            n = 1 + 6 * i
            half(n, (2, 3, 4), 2 * i, summing)
            half(n + 3, (5, 0, 1), 2 * i + 1, summing)
            return carry

        return turn

    lax.fori_loop(0, LAG // 2, turns(False), 0)
    lax.fori_loop(LAG // 2, TRIPS, turns(True), 0)

    def rest(i, carry):
        n = 1 + 6 * i
        arrived(n, 3, 2 * i)
        arrived(n + 3, 3, 2 * i + 1)
        add_up([n, n + 1, n + 2])
        add_up([n + 3, n + 4, n + 5])
        return carry

    lax.fori_loop(TRIPS - LAG // 2, TRIPS, rest, 0)
    arrived(ND - 1, 1, 2 * TRIPS)
    add_up([0, ND - 1])

    for copy in part_copies:
        copy.wait_recv()
    for h in range(HI):
        lanes = slice(128 * h, 128 * h + 128)
        evolved = part[0, :, lanes]
        for k in range(1, N_COL):
            evolved = evolved + gains[k, :, lanes]
        miss_out[:, lanes] = evolved - acc[16 * h : 16 * h + 16, :] * (1.0 / NSAMP)

    for g in range(SLOTS):
        fetch(0, g).wait()
    for copy in edge_copies + part_copies:
        copy.wait_send()
    pltpu.make_async_copy(send.at[pl.ds(1, ND - 1)], recv.at[pl.ds(1, ND - 1)], send_sem).wait()


def body(disk, response, spectra, srf, send_pix, recv_foot):
    vmem = pl.BlockSpec(memory_space=pltpu.VMEM)
    hbm = pl.BlockSpec(memory_space=pl.ANY)

    turned = jnp.transpose(disk, (1, 0, 2))
    wide = response.astype(F32)
    taps = jnp.concatenate([wide[:, :1], jnp.zeros((KS, 256 - KS), F32), wide[:, :0:-1]], axis=1)

    slot = lax.rem(lax.iota(jnp.int32, ND * CAP), jnp.int32(CAP)) // ROWS
    cell = ((send_pix >> 12) << 9) | (send_pix & 511)
    idx = (((slot - (send_pix >> 9)) & 7) << 13) | cell
    idx = jnp.pad(idx.reshape(ND, 1, CAP), ((0, 0), (0, 0), (0, 384 - CAP)))

    foot = recv_foot.reshape(ND, UNITS, ROWS)
    foot = jnp.pad(foot, ((0, 0), (0, 0), (0, 128 - ROWS)), constant_values=FPD)

    dma = pltpu.SemaphoreType.DMA
    return tuple(
        pl.pallas_call(
            kernel,
            out_shape=(
                jax.ShapeDtypeStruct((BANDS, TR, TC), BF16),
                jax.ShapeDtypeStruct((BANDS, FPD), F32),
            ),
            in_specs=[hbm, vmem, vmem, hbm, hbm, vmem],
            out_specs=(vmem, vmem),
            scratch_shapes=[
                pltpu.VMEM((TR, BANDS, TC), BF16),
                pltpu.VMEM((74, 2, BANDS, 640), BF16),
                pltpu.VMEM((KS + 2, 256, 128), BF16),
                pltpu.VMEM((N_COL, 512, FPD), BF16),
                pltpu.VMEM((N_COL, BANDS, FPD), F32),
                pltpu.VMEM((N_COL, BANDS, FPD), F32),
                pltpu.VMEM((2, 16, BANDS, 128), BF16),
                pltpu.VMEM((2, EDGE, BANDS, TC), BF16),
                pltpu.VMEM((2, 16, BANDS, 128), BF16),
                pltpu.VMEM((4, 2, BANDS, 128), BF16),
                pltpu.VMEM((512, 256), F32),
                pltpu.VMEM((4, 256, 128), F32),
                pltpu.VMEM((UNITS * CELLS, 128), F32),
                pltpu.VMEM((SLOTS, PADR, 128), F32),
                pltpu.VMEM((ND, PADR, 128), BF16),
                pltpu.VMEM((ND, PADR, 128), BF16),
                pltpu.VMEM((HI * BANDS, 128), F32),
                pltpu.SMEM((SLOTS, 1, 384), jnp.int32),
                dma,
                dma((N_COL,)),
                dma((SLOTS,)),
                dma((8,)),
                dma((8,)),
                dma((N_COL,)),
                dma((N_COL,)),
                dma,
                dma((2 * TRIPS + 1,)),
            ],
            compiler_params=pltpu.CompilerParams(
                vmem_limit_bytes=60 << 20, collective_id=0, has_side_effects=True
            ),
            cost_estimate=pl.CostEstimate(flops=16 << 30, bytes_accessed=16 << 20, transcendentals=0),
            name="collocate",
        )(turned, taps, srf, spectra, idx, foot)
    )


def solution(mesh):
    placed = (
        P(None, "row", "col"),
        P(),
        P("col", "row"),
        P(None, "col"),
        P(("row", "col")),
        P(("row", "col")),
    )
    return jax.shard_map(
        body,
        mesh=mesh,
        in_specs=placed,
        out_specs=(P(None, "row", "col"), P(None, ("row", "col"))),
        check_vma=False,
    )
```

time: 704 us -> 92.6 us (0.13)
  local copies, waits for them, and re-layouts: 461 us -> 11.5 us
  matrix products: 154 us -> 0 us
  Pallas kernels: 0 us -> 77.3 us
  starting transfers between devices: 23.5 us -> 0 us
  waiting for transfers between devices: 22.7 us -> 0 us
  other arithmetic: 23.5 us -> 1.77 us
  between operations: 14.3 us -> 0.68 us
    dot_general x22 -> x0, matrix products: 154 us -> none  [the longest x19 127 us: add_offset(): jnp.dot(taken.reshape(-1, window), banded[offset_row], preferred_element_...]
    reshape x19 -> x2, local copies, waits for them, and re-layouts: 145 us -> 1.83 us  [the longest x1 1.53 us: body(): foot = recv_foot.reshape(ND, UNITS, ROWS)]
    gather x2 -> x0, local copies, waits for them, and re-layouts: 140 us -> none  [body(): outgoing = jnp.take(flat_tile, send_pix, axis=1)]
    dynamic_slice x38 -> x0, local copies, waits for them, and re-layouts: 126 us -> none  [add_offset(): taken = lax.dynamic_slice_in_dim(stacked, offset_row, tile_rows, axis=1)]
    pallas_call x0 -> x1, Pallas kernels: none -> 77.3 us  [body(): pl.pallas_call(kernel, out_shape=(jax.ShapeDtypeStruct((BANDS, TR, TC), B...]
    all_to_all x1 -> x0, waiting for transfers between devices: 22.3 us -> none  [body(): lax.all_to_all(outgoing, ('row', 'col'), split_axis=1, concat_axis=1, til...]
    mul x2 -> x0, local copies, waits for them, and re-layouts: 17.3 us -> none  [body(): incoming[:, None, :] * high_table[None, :, :]]
    convert_element_type x3 -> x0, local copies, waits for them, and re-layouts: 16.8 us -> none  [body(): running.reshape(band_count, tile_rows, tile_cols).astype(jnp.bfloat16)]
  transfers between devices with their start and end apart: 6 -> 0, of which waited for: 2 -> 0; matrix products, arithmetic and copies ran while one was open for 91% -> 0% of each run, Pallas kernels for 0% -> 0%
where the time goes in v2:
time: 92.6 us; the launch traced here: 91.3 us
  Pallas kernels  77.3 us (83%)
  local copies, waits for them, and re-layouts  11.5 us (12%)
  other arithmetic  1.77 us (2%)
    pallas_call x1, Pallas kernels, body(): pl.pallas_call(kernel, out_shape=(jax.ShapeDtypeStruct((BANDS, TR, TC), B...  77.3 us
    unnamed x7, local copies, waits for them, and re-layouts  6.26 us

profile of v2, /device:TPU:1, one launch (start us, length us, event | category | flops | bytes accessed | tf_op | source)
XLA Modules:
  0.0 91.3 jit_solution(793460587153322341)
XLA Ops:
  0.6 0.0 copy-start
  0.6 0.1 pad.11.clone
  0.7 0.9 slice.9
  1.6 0.1 rev.3
  1.7 0.7 slice.8
  2.4 0.7 pad_maximum_fusion.taps
  3.1 1.1 %fusion.3 = s32[36864]{0:T(1024)S(1)} fusion(s32[36864]{0:T(1024)} %param.10), kind=kLoop, calls=%fused_computation.5 | loop fusion | flops 663552 | bytes 294912 | tf_op jit(solution)/shard_map/or | solution.py:348
  4.2 0.3 reshape.12
  4.5 0.8 pad.8.idx_ref
  5.3 1.5 %reshape.11 = s32[128,8,36]{2,1,0:T(8,128)S(1)} reshape(s32[36864]{0:T(1024)} %param.11) | data formatting | bytes 294912 | tf_op jit(solution)/shard_map/reshape | solution.py:351
  6.8 0.8 pad.9.foot_ref
  7.7 0.0 copy-done
  7.7 2.5 %copy.12 = bf16[16,128,512]{2,0,1:T(8,128)(2,1)} copy(bf16[16,128,512]{2,1,0:T(8,128)(2,1)S(1)} %copy-done) | data formatting | bytes 4194304 | tf_op args[0]
  10.1 77.3 %collocate.1 = (bf16[16,128,512]{2,1,0:T(8,128)(2,1)}, f32[16,1536]{1,0:T(8,128)}) custom-call(bf16[128,16,512]{2,1,0:T(8,128)(2,1)} %bitcast.3, f32[19,256]{1,0:T(8,128)} %pad_maximum_fusion.taps, bf16[16,512]{1,0:T(8,128)(2,1)} %srf_ref.1, bf16[512,6144]{1,0:T(8,128)(2,1)} %spectra.1, s32[128,1,384]{2,1,0:T(1,128)} %pad.8.idx_ref, s32[128,8,128]{2,1,0:T(8,128)} %pad.9.foot_ref), custom_call_target="tpu_custom_call" | custom-call | flops 17179869184 | bytes 16777216 | tf_op jit(solution)/shard_map/collocate/pallas_call | solution.py:356
  87.5 0.0 copy-start.1
  87.5 3.1 %copy.15 = bf16[16,128,512]{2,1,0:T(8,128)(2,1)} copy(bf16[16,128,512]{2,1,0:T(8,128)(2,1)} %get-tuple-element.4) | data formatting | bytes 4194304
  90.6 0.0 copy-done.1
  90.6 0.6 copy.16
  (1 shorter events, 0.0 us)
Async XLA Ops:
  0.6 7.0 %copy-start = (bf16[16,128,512]{2,1,0:T(8,128)(2,1)S(1)}, bf16[16,128,512]{2,1,0:T(8,128)(2,1)}, u32[]{:S(2)}) copy-start(bf16[16,128,512]{2,1,0:T(8,128)(2,1)} %param.6) | copy-start | bytes 6291460
  87.5 3.1 %copy-start.1 = (f32[16,1536]{1,0:T(8,128)S(1)}, f32[16,1536]{1,0:T(8,128)}, u32[]{:S(2)}) copy-start(f32[16,1536]{1,0:T(8,128)} %get-tuple-element.5) | copy-start | bytes 294916

commit v3 on v2

--- a/solution.py
+++ b/solution.py
@@ -21,9 +21,11 @@
 PADR = 40
 CELLS = TR // 8 * TC
 HI = FPD // 128
-SLOTS = 6
+BATCH = 3
+SLOTS = 2 * BATCH
 TRIPS = 21
-LAG = 8
+LAG = 12
+TRIOS = 2 * TRIPS
 MESH = pl.DeviceIdType.MESH
 F32 = jnp.float32
 BF16 = jnp.bfloat16
@@ -31,15 +33,16 @@
 
 def kernel(
     turned, taps, srf_ref, spectra, idx_ref, foot_ref, blur_out, miss_out,
-    own, p_ref, w_ref, spec, part, gains, edge, hrow, hcol, hcor, accb, s_ref, rot, stage, send, recv,
-    acc, sm, own_sem, spec_sem, idx_sem, edge_send, edge_recv, part_send, part_recv, send_sem, recv_sem,
+    own, p_ref, w_ref, lines, spec, part, gains, edge, hrow, hcol, hcor, accb, s_ref, rot, stage, send, recv,
+    acc, sm, ring, own_sem, spec_sem, idx_sem, edge_send, edge_recv, part_send, part_recv, send_sem, recv_sem,
 ):
     row = lax.axis_index("row")
     col = lax.axis_index("col")
     me = row * N_COL + col
 
     def place(d):
-        return (d // N_COL, lax.rem(d, N_COL))
+        r = lax.div(d, N_COL)
+        return (r, d - r * N_COL)
 
     own_copy = pltpu.make_async_copy(turned, own, own_sem)
     own_copy.start()
@@ -59,13 +62,23 @@
     for g in range(SLOTS):
         fetch((0, ND - 1)[g] if g < 2 else step_of(g), g).start()
 
+    def around(value, by, count):
+        moved = value + by
+        return jnp.where(moved >= count, moved - count, jnp.where(moved < 0, moved + count, moved))
+
     barrier = pltpu.get_barrier_semaphore()
-
-    def greet(i, carry):
-        pl.semaphore_signal(barrier, inc=1, device_id=place(lax.rem(me + i, ND)), device_id_type=MESH)
-        return carry
-
-    lax.fori_loop(1, ND, greet, 0)
+    for dr, dc in [(0, 1), (0, 2), (0, 3)] + [(dr, dc) for dr in (1, -1) for dc in range(N_COL)]:
+        there = (around(row, dr, N_ROW), around(col, dc, N_COL))
+        pl.semaphore_signal(barrier, inc=1, device_id=there, device_id_type=MESH)
+
+    def ring_tell(level):
+        for by in (1 << level, -(1 << level)):
+            pl.semaphore_signal(
+                ring.at[level], inc=1, device_id=(around(row, by, N_ROW), col), device_id_type=MESH
+            )
+
+    def ring_hear(level):
+        pl.semaphore_wait(ring.at[level], 2)
 
     lane = lax.broadcasted_iota(jnp.int32, (BANDS, 128), 1)
     own_copy.wait()
@@ -83,7 +96,7 @@
         return carry
 
     lax.fori_loop(0, TR // 8, pack, 0)
-    pl.semaphore_wait(barrier, ND - 1)
+    pl.semaphore_wait(barrier, 2 * N_COL + N_COL - 1)
 
     up, down = lax.rem(row + N_ROW - 1, N_ROW), lax.rem(row + 1, N_ROW)
     west, east = lax.rem(col + N_COL - 1, N_COL), lax.rem(col + 1, N_COL)
@@ -106,6 +119,7 @@
     ]
     for copy in edge_copies:
         copy.start()
+    ring_tell(0)
 
     part_copies = []
     for k, copy in spec_copies:
@@ -122,8 +136,13 @@
     w_ref[0] = jnp.zeros((256, 128), BF16)
     w_ref[KS + 1] = jnp.zeros((256, 128), BF16)
 
+    tap = lax.broadcasted_iota(jnp.int32, (128, 256), 0)
+    at = lax.broadcasted_iota(jnp.int32, (128, 256), 1)
+    flip = jnp.where((tap + at == 256) | ((tap == 0) & (at == 0)), 1.0, 0.0).astype(BF16)
+    lines[...] = jnp.dot(taps[...], flip, preferred_element_type=F32)
+
     def band(a, carry):
-        line = jnp.broadcast_to(taps[pl.ds(a, 1), :], (256, 256))
+        line = jnp.broadcast_to(lines[pl.ds(a, 1), :], (256, 256))
         w_ref[a + 1] = pltpu.roll(line, 0, 1, stride=1, stride_axis=0)[:, :128].astype(BF16)
         return carry
 
@@ -146,6 +165,8 @@
 
     for copy in edge_copies:
         copy.wait_recv()
+    ring_hear(0)
+    ring_tell(1)
 
     has_up, has_down = row > 0, row < N_ROW - 1
     has_west, has_east = col > 0, col < N_COL - 1
@@ -200,13 +221,13 @@
     def settle(yb):
         rounded = accb[...].astype(BF16).astype(F32)
         for j in range(4):
-            lines = [
+            strips = [
                 rounded[j * 128 + m * 16 : j * 128 + m * 16 + 16, q * 128 : q * 128 + 128]
                 for m in range(8)
                 for q in range(2)
             ]
             for h in range(2):
-                piece = jnp.concatenate(lines[8 * h : 8 * h + 8], axis=0)
+                piece = jnp.concatenate(strips[8 * h : 8 * h + 8], axis=0)
                 s_ref[j, pl.ds(h * 128, 128), :] = piece
                 cells = jnp.transpose(piece)
                 for t in range(UNITS):
@@ -218,13 +239,19 @@
                 ].astype(BF16)
 
     accb[...] = products(0)
+    ring_hear(1)
+    ring_tell(2)
 
     def block(yb, carry):
         settle(yb - 1)
         accb[...] = products(yb)
         return carry
 
-    lax.fori_loop(1, TR // 16, block, 0)
+    lax.fori_loop(1, 3, block, 0)
+    ring_hear(2)
+    ring_tell(3)
+    lax.fori_loop(3, TR // 16, block, 0)
+    ring_hear(3)
     settle(TR // 16 - 1)
 
     stage[...] = jnp.zeros(stage.shape, F32)
@@ -277,29 +304,38 @@
         fetch(n, g).wait()
         if n:
             send[n] = gather(g)
-            message(n, 2 * TRIPS).start()
+            message(n, TRIOS).start()
         else:
             recv[0] = gather(g)
         fetch(step_of(g + SLOTS), g).start()
 
-    def half(n, groups, trio, summing):
-        for k, g in enumerate(groups):
+    def sums(first, waiting):
+        trio = lax.div(first, 3)
+        if waiting:
+            arrived(first, 3, trio)
+        add_up([first, first + 1, first + 2])
+
+    def segment(n, slots, summing):
+        trio = lax.div(n, 3)
+        for k, g in enumerate(slots):
             fetch(n + k, g).wait()
         if summing:
-            back = n - 3 * LAG
-            arrived(back, 3, trio - LAG)
-            add_up([back, back + 1, back + 2])
-        for k, g in enumerate(groups):
+            sums(n - BATCH * LAG, True)
+        for k, g in enumerate(slots):
             send[n + k] = gather(g)
-        for k, g in enumerate(groups):
+        for k, g in enumerate(slots):
+            fetch(jnp.minimum(n + k + SLOTS, ND - 1), g).start()
+        for k in range(BATCH):
             message(n + k, trio).start()
-            fetch(jnp.minimum(n + k + SLOTS, ND - 1), g).start()
+
+    early = tuple(range(2, 2 + BATCH))
+    late = tuple((2 + BATCH + k) % SLOTS for k in range(BATCH))
 
     def turns(summing):
         def turn(i, carry):
-            n = 1 + 6 * i
-            half(n, (2, 3, 4), 2 * i, summing)
-            half(n + 3, (5, 0, 1), 2 * i + 1, summing)
+            n = 1 + 2 * BATCH * i
+            segment(n, early, summing)
+            segment(n + BATCH, late, summing)
             return carry
 
         return turn
@@ -308,15 +344,11 @@
     lax.fori_loop(LAG // 2, TRIPS, turns(True), 0)
 
     def rest(i, carry):
-        n = 1 + 6 * i
-        arrived(n, 3, 2 * i)
-        arrived(n + 3, 3, 2 * i + 1)
-        add_up([n, n + 1, n + 2])
-        add_up([n + 3, n + 4, n + 5])
-        return carry
-
-    lax.fori_loop(TRIPS - LAG // 2, TRIPS, rest, 0)
-    arrived(ND - 1, 1, 2 * TRIPS)
+        sums(1 + BATCH * i, True)
+        return carry
+
+    lax.fori_loop(2 * TRIPS - LAG, 2 * TRIPS, rest, 0)
+    arrived(ND - 1, 1, TRIOS)
     add_up([0, ND - 1])
 
     for copy in part_copies:
@@ -340,13 +372,11 @@
     hbm = pl.BlockSpec(memory_space=pl.ANY)
 
     turned = jnp.transpose(disk, (1, 0, 2))
-    wide = response.astype(F32)
-    taps = jnp.concatenate([wide[:, :1], jnp.zeros((KS, 256 - KS), F32), wide[:, :0:-1]], axis=1)
-
-    slot = lax.rem(lax.iota(jnp.int32, ND * CAP), jnp.int32(CAP)) // ROWS
-    cell = ((send_pix >> 12) << 9) | (send_pix & 511)
-    idx = (((slot - (send_pix >> 9)) & 7) << 13) | cell
-    idx = jnp.pad(idx.reshape(ND, 1, CAP), ((0, 0), (0, 0), (0, 384 - CAP)))
+    taps = jnp.pad(response, ((0, 24 - KS), (0, 128 - KS)))
+
+    pix = jnp.pad(send_pix.reshape(ND, 1, CAP), ((0, 0), (0, 0), (0, 384 - CAP)))
+    slot = lax.broadcasted_iota(jnp.int32, pix.shape, 2) // ROWS
+    idx = (((slot - (pix >> 9)) & 7) << 13) | ((pix >> 12) << 9) | (pix & 511)
 
     foot = recv_foot.reshape(ND, UNITS, ROWS)
     foot = jnp.pad(foot, ((0, 0), (0, 0), (0, 128 - ROWS)), constant_values=FPD)
@@ -365,6 +395,7 @@
                 pltpu.VMEM((TR, BANDS, TC), BF16),
                 pltpu.VMEM((74, 2, BANDS, 640), BF16),
                 pltpu.VMEM((KS + 2, 256, 128), BF16),
+                pltpu.VMEM((24, 256), F32),
                 pltpu.VMEM((N_COL, 512, FPD), BF16),
                 pltpu.VMEM((N_COL, BANDS, FPD), F32),
                 pltpu.VMEM((N_COL, BANDS, FPD), F32),
@@ -380,6 +411,7 @@
                 pltpu.VMEM((ND, PADR, 128), BF16),
                 pltpu.VMEM((HI * BANDS, 128), F32),
                 pltpu.SMEM((SLOTS, 1, 384), jnp.int32),
+                pltpu.SemaphoreType.REGULAR((4,)),
                 dma,
                 dma((N_COL,)),
                 dma((SLOTS,)),
@@ -388,7 +420,7 @@
                 dma((N_COL,)),
                 dma((N_COL,)),
                 dma,
-                dma((2 * TRIPS + 1,)),
+                dma((TRIOS + 1,)),
             ],
             compiler_params=pltpu.CompilerParams(
                 vmem_limit_bytes=60 << 20, collective_id=0, has_side_effects=True

time: 92.6 us -> 87 us (0.940)
  Pallas kernels: 77.3 us -> 73.4 us
    pallas_call x1, Pallas kernels: 77.3 us -> 73.4 us  [body(): pl.pallas_call(kernel, out_shape=(jax.ShapeDtypeStruct((BANDS, TR, TC), B...]
    slice x2 -> x0, local copies, waits for them, and re-layouts: 1.59 us -> none  [the longest x1 0.9 us: body(): wide[:, :0:-1]]
where the time goes in v3:
time: 87 us; the launch traced here: 86.6 us
  Pallas kernels  73.4 us (84%)
  local copies, waits for them, and re-layouts  11.3 us (13%)
  other arithmetic  1.18 us (1%)
    pallas_call x1, Pallas kernels, body(): pl.pallas_call(kernel, out_shape=(jax.ShapeDtypeStruct((BANDS, TR, TC), B...  73.4 us
    unnamed x7, local copies, waits for them, and re-layouts  6.26 us

profile of v3, /device:TPU:1, one launch (start us, length us, event | category | flops | bytes accessed | tf_op | source)
XLA Modules:
  0.0 86.6 jit_solution(67299753106286356)
XLA Ops:
  0.6 0.0 copy-start
  0.7 1.4 %pad.12.taps = bf16[24,128]{1,0:T(8,128)(2,1)} pad(bf16[19,19]{1,0:T(8,128)(2,1)} %param.7, bf16[]{:T(256)} %constant.5.clone.1), padding=0_5x0_109 | pad | bytes 6868 | tf_op jit(solution)/shard_map/jit(_pad)/pad | solution.py:375
  2.1 1.2 %reshape.70 = s32[128,1,288]{2,1,0:T(1,128)S(1)} reshape(s32[36864]{0:T(1024)} %param.10) | data formatting | bytes 294912 | tf_op jit(solution)/shard_map/reshape | solution.py:377
  3.3 1.2 %and_or_fusion.idx_ref = s32[128,1,384]{2,1,0:T(1,128)} fusion(pred[384]{0:T(512)(128)(4,1)S(1)} %fusion.4, s32[128,1,288]{2,1,0:T(1,128)S(1)} %reshape.70, s32[384]{0:T(512)S(1)} %get-tuple-element.2, s32[384]{0:T(512)S(1)} %get-tuple-element.3), kind=kLoop, calls=%fused_computation.4 | loop fusion | flops 491520 | bytes 347520 | tf_op jit(solution)/shard_map/or | solution.py:379
  4.5 1.5 %reshape.69 = s32[128,8,36]{2,1,0:T(8,128)S(1)} reshape(s32[36864]{0:T(1024)} %param.11) | data formatting | bytes 294912 | tf_op jit(solution)/shard_map/reshape | solution.py:381
  6.0 0.8 pad.14.foot_ref
  6.9 0.0 copy-done
  6.9 2.5 %copy.16 = bf16[16,128,512]{2,0,1:T(8,128)(2,1)} copy(bf16[16,128,512]{2,1,0:T(8,128)(2,1)S(1)} %copy-done) | data formatting | bytes 4194304 | tf_op args[0]
  9.3 73.4 %collocate.1 = (bf16[16,128,512]{2,1,0:T(8,128)(2,1)}, f32[16,1536]{1,0:T(8,128)}) custom-call(bf16[128,16,512]{2,1,0:T(8,128)(2,1)} %bitcast.3, bf16[24,128]{1,0:T(8,128)(2,1)} %pad.12.taps, bf16[16,512]{1,0:T(8,128)(2,1)} %srf_ref.1, bf16[512,6144]{1,0:T(8,128)(2,1)} %spectra.1, s32[128,1,384]{2,1,0:T(1,128)} %and_or_fusion.idx_ref, ...), custom_call_target="tpu_custom_call" | custom-call | flops 17179869184 | bytes 16777216 | tf_op jit(solution)/shard_map/collocate/pallas_call | solution.py:386
  82.8 0.0 copy-start.1
  82.8 3.1 %copy.19 = bf16[16,128,512]{2,1,0:T(8,128)(2,1)} copy(bf16[16,128,512]{2,1,0:T(8,128)(2,1)} %get-tuple-element.6) | data formatting | bytes 4194304
  85.9 0.0 copy-done.1
  85.9 0.6 copy.20
  (2 shorter events, 0.0 us)
Async XLA Ops:
  0.6 6.2 %copy-start = (bf16[16,128,512]{2,1,0:T(8,128)(2,1)S(1)}, bf16[16,128,512]{2,1,0:T(8,128)(2,1)}, u32[]{:S(2)}) copy-start(bf16[16,128,512]{2,1,0:T(8,128)(2,1)} %param.6) | copy-start | bytes 6291460
  82.8 3.1 %copy-start.1 = (f32[16,1536]{1,0:T(8,128)S(1)}, f32[16,1536]{1,0:T(8,128)}, u32[]{:S(2)}) copy-start(f32[16,1536]{1,0:T(8,128)} %get-tuple-element.7) | copy-start | bytes 294916

commit v4 on v3

--- a/solution.py
+++ b/solution.py
@@ -21,20 +21,20 @@
 PADR = 40
 CELLS = TR // 8 * TC
 HI = FPD // 128
-BATCH = 3
+BATCH = 6
 SLOTS = 2 * BATCH
-TRIPS = 21
-LAG = 12
-TRIOS = 2 * TRIPS
+TRIPS = 10
+LAG = 8
+TRIOS = 2 * (2 * TRIPS + 1)
 MESH = pl.DeviceIdType.MESH
 F32 = jnp.float32
 BF16 = jnp.bfloat16
 
 
 def kernel(
-    turned, taps, srf_ref, spectra, idx_ref, foot_ref, blur_out, miss_out,
-    own, p_ref, w_ref, lines, spec, part, gains, edge, hrow, hcol, hcor, accb, s_ref, rot, stage, send, recv,
-    acc, sm, ring, own_sem, spec_sem, idx_sem, edge_send, edge_recv, part_send, part_recv, send_sem, recv_sem,
+    turned, taps, srf_ref, spectra, idx_ref, feet, blur_out, miss_out,
+    own, p_ref, w_ref, lines, spec, part, gains, edge, hrow, hcol, hcor, accb, foot_ref, rot, stage, send, recv,
+    acc, sm, ring, own_sem, out_sem, foot_sem, spec_sem, idx_sem, edge_send, edge_recv, part_send, part_recv, send_sem, recv_sem,
 ):
     row = lax.axis_index("row")
     col = lax.axis_index("col")
@@ -46,6 +46,8 @@
 
     own_copy = pltpu.make_async_copy(turned, own, own_sem)
     own_copy.start()
+    foot_copy = pltpu.make_async_copy(feet, foot_ref, foot_sem)
+    foot_copy.start()
     spec_copies = []
     for k in (1, 2, 3, 0):
         at = pl.multiple_of(lax.rem(col + k, N_COL) * FPD, 128)
@@ -219,26 +221,24 @@
         return total
 
     def settle(yb):
-        rounded = accb[...].astype(BF16).astype(F32)
+        kept = accb[...].astype(BF16)
+        rounded = kept.astype(F32)
         for j in range(4):
-            strips = [
-                rounded[j * 128 + m * 16 : j * 128 + m * 16 + 16, q * 128 : q * 128 + 128]
-                for m in range(8)
-                for q in range(2)
-            ]
+            strips = []
+            for m in range(8):
+                for q in range(2):
+                    part_of = (slice(j * 128 + m * 16, j * 128 + m * 16 + 16), slice(q * 128, q * 128 + 128))
+                    strips.append(rounded[part_of])
+                    own[yb * 16 + 2 * m + q, :, j * 128 : j * 128 + 128] = kept[part_of]
             for h in range(2):
-                piece = jnp.concatenate(strips[8 * h : 8 * h + 8], axis=0)
-                s_ref[j, pl.ds(h * 128, 128), :] = piece
-                cells = jnp.transpose(piece)
+                cells = jnp.transpose(jnp.concatenate(strips[8 * h : 8 * h + 8], axis=0))
                 for t in range(UNITS):
                     at = pl.multiple_of(t * CELLS + (2 * yb + h) * TC + j * 128, 128)
                     rot[pl.ds(at, 128), :] = pltpu.roll(cells, 16 * t, 1) if t else cells
-            for b in range(BANDS):
-                blur_out[b, pl.ds(pl.multiple_of(yb * 16, 16), 16), j * 128 : j * 128 + 128] = s_ref[
-                    j, pl.ds(b, 16, stride=16), :
-                ].astype(BF16)
 
     accb[...] = products(0)
+    for copy in edge_copies:
+        copy.wait_send()
     ring_hear(1)
     ring_tell(2)
 
@@ -253,6 +253,9 @@
     lax.fori_loop(3, TR // 16, block, 0)
     ring_hear(3)
     settle(TR // 16 - 1)
+    out_copy = pltpu.make_async_copy(own, blur_out, out_sem)
+    out_copy.start()
+    foot_copy.wait()
 
     stage[...] = jnp.zeros(stage.shape, F32)
     acc[...] = jnp.zeros(acc.shape, F32)
@@ -313,7 +316,9 @@
         trio = lax.div(first, 3)
         if waiting:
             arrived(first, 3, trio)
+            arrived(first + 3, 3, trio + 1)
         add_up([first, first + 1, first + 2])
+        add_up([first + 3, first + 4, first + 5])
 
     def segment(n, slots, summing):
         trio = lax.div(n, 3)
@@ -326,7 +331,7 @@
         for k, g in enumerate(slots):
             fetch(jnp.minimum(n + k + SLOTS, ND - 1), g).start()
         for k in range(BATCH):
-            message(n + k, trio).start()
+            message(n + k, trio + k // 3).start()
 
     early = tuple(range(2, 2 + BATCH))
     late = tuple((2 + BATCH + k) % SLOTS for k in range(BATCH))
@@ -342,12 +347,13 @@
 
     lax.fori_loop(0, LAG // 2, turns(False), 0)
     lax.fori_loop(LAG // 2, TRIPS, turns(True), 0)
+    segment(1 + 2 * BATCH * TRIPS, early, True)
 
     def rest(i, carry):
         sums(1 + BATCH * i, True)
         return carry
 
-    lax.fori_loop(2 * TRIPS - LAG, 2 * TRIPS, rest, 0)
+    lax.fori_loop(2 * TRIPS + 1 - LAG, 2 * TRIPS + 1, rest, 0)
     arrived(ND - 1, 1, TRIOS)
     add_up([0, ND - 1])
 
@@ -362,8 +368,9 @@
 
     for g in range(SLOTS):
         fetch(0, g).wait()
-    for copy in edge_copies + part_copies:
+    for copy in part_copies:
         copy.wait_send()
+    out_copy.wait()
     pltpu.make_async_copy(send.at[pl.ds(1, ND - 1)], recv.at[pl.ds(1, ND - 1)], send_sem).wait()
 
 
@@ -382,53 +389,54 @@
     foot = jnp.pad(foot, ((0, 0), (0, 0), (0, 128 - ROWS)), constant_values=FPD)
 
     dma = pltpu.SemaphoreType.DMA
-    return tuple(
-        pl.pallas_call(
-            kernel,
-            out_shape=(
-                jax.ShapeDtypeStruct((BANDS, TR, TC), BF16),
-                jax.ShapeDtypeStruct((BANDS, FPD), F32),
-            ),
-            in_specs=[hbm, vmem, vmem, hbm, hbm, vmem],
-            out_specs=(vmem, vmem),
-            scratch_shapes=[
-                pltpu.VMEM((TR, BANDS, TC), BF16),
-                pltpu.VMEM((74, 2, BANDS, 640), BF16),
-                pltpu.VMEM((KS + 2, 256, 128), BF16),
-                pltpu.VMEM((24, 256), F32),
-                pltpu.VMEM((N_COL, 512, FPD), BF16),
-                pltpu.VMEM((N_COL, BANDS, FPD), F32),
-                pltpu.VMEM((N_COL, BANDS, FPD), F32),
-                pltpu.VMEM((2, 16, BANDS, 128), BF16),
-                pltpu.VMEM((2, EDGE, BANDS, TC), BF16),
-                pltpu.VMEM((2, 16, BANDS, 128), BF16),
-                pltpu.VMEM((4, 2, BANDS, 128), BF16),
-                pltpu.VMEM((512, 256), F32),
-                pltpu.VMEM((4, 256, 128), F32),
-                pltpu.VMEM((UNITS * CELLS, 128), F32),
-                pltpu.VMEM((SLOTS, PADR, 128), F32),
-                pltpu.VMEM((ND, PADR, 128), BF16),
-                pltpu.VMEM((ND, PADR, 128), BF16),
-                pltpu.VMEM((HI * BANDS, 128), F32),
-                pltpu.SMEM((SLOTS, 1, 384), jnp.int32),
-                pltpu.SemaphoreType.REGULAR((4,)),
-                dma,
-                dma((N_COL,)),
-                dma((SLOTS,)),
-                dma((8,)),
-                dma((8,)),
-                dma((N_COL,)),
-                dma((N_COL,)),
-                dma,
-                dma((TRIOS + 1,)),
-            ],
-            compiler_params=pltpu.CompilerParams(
-                vmem_limit_bytes=60 << 20, collective_id=0, has_side_effects=True
-            ),
-            cost_estimate=pl.CostEstimate(flops=16 << 30, bytes_accessed=16 << 20, transcendentals=0),
-            name="collocate",
-        )(turned, taps, srf, spectra, idx, foot)
-    )
+    blurred, mismatch = pl.pallas_call(
+        kernel,
+        out_shape=(
+            jax.ShapeDtypeStruct((TR, BANDS, TC), BF16),
+            jax.ShapeDtypeStruct((BANDS, FPD), F32),
+        ),
+        in_specs=[hbm, vmem, vmem, hbm, hbm, hbm],
+        out_specs=(hbm, vmem),
+        scratch_shapes=[
+            pltpu.VMEM((TR, BANDS, TC), BF16),
+            pltpu.VMEM((74, 2, BANDS, 640), BF16),
+            pltpu.VMEM((KS + 2, 256, 128), BF16),
+            pltpu.VMEM((24, 256), F32),
+            pltpu.VMEM((N_COL, 512, FPD), BF16),
+            pltpu.VMEM((N_COL, BANDS, FPD), F32),
+            pltpu.VMEM((N_COL, BANDS, FPD), F32),
+            pltpu.VMEM((2, 16, BANDS, 128), BF16),
+            pltpu.VMEM((2, EDGE, BANDS, TC), BF16),
+            pltpu.VMEM((2, 16, BANDS, 128), BF16),
+            pltpu.VMEM((4, 2, BANDS, 128), BF16),
+            pltpu.VMEM((512, 256), F32),
+            pltpu.VMEM((ND, UNITS, 128), jnp.int32),
+            pltpu.VMEM((UNITS * CELLS, 128), F32),
+            pltpu.VMEM((SLOTS, PADR, 128), F32),
+            pltpu.VMEM((ND, PADR, 128), BF16),
+            pltpu.VMEM((ND, PADR, 128), BF16),
+            pltpu.VMEM((HI * BANDS, 128), F32),
+            pltpu.SMEM((SLOTS, 1, 384), jnp.int32),
+            pltpu.SemaphoreType.REGULAR((4,)),
+            dma,
+            dma,
+            dma,
+            dma((N_COL,)),
+            dma((SLOTS,)),
+            dma((8,)),
+            dma((8,)),
+            dma((N_COL,)),
+            dma((N_COL,)),
+            dma,
+            dma((TRIOS + 1,)),
+        ],
+        compiler_params=pltpu.CompilerParams(
+            vmem_limit_bytes=60 << 20, collective_id=0, has_side_effects=True
+        ),
+        cost_estimate=pl.CostEstimate(flops=16 << 30, bytes_accessed=16 << 20, transcendentals=0),
+        name="collocate",
+    )(turned, taps, srf, spectra, idx, foot)
+    return jnp.transpose(blurred, (1, 0, 2)), mismatch
 
 
 def solution(mesh):

time: 87 us -> 80.9 us (0.930)
  Pallas kernels: 73.4 us -> 66.6 us
  local copies, waits for them, and re-layouts: 11.3 us -> 12.2 us
    pallas_call x1, Pallas kernels: 73.4 us -> 66.6 us  [body(): pl.pallas_call(kernel, out_shape=(jax.ShapeDtypeStruct((TR, BANDS, TC), B...]
    unnamed x7, local copies, waits for them, and re-layouts: 6.26 us -> 7.23 us
where the time goes in v4:
time: 80.9 us; the launch traced here: 80.7 us
  Pallas kernels  66.6 us (82%)
  local copies, waits for them, and re-layouts  12.2 us (15%)
  other arithmetic  1.18 us (1%)
    pallas_call x1, Pallas kernels, body(): pl.pallas_call(kernel, out_shape=(jax.ShapeDtypeStruct((TR, BANDS, TC), B...  66.6 us
    unnamed x7, local copies, waits for them, and re-layouts  7.23 us

profile of v4, /device:TPU:1, one launch (start us, length us, event | category | flops | bytes accessed | tf_op | source)
XLA Modules:
  0.0 80.7 jit_solution(709737655796947211)
XLA Ops:
  0.6 0.0 copy-start
  0.7 1.4 %pad.12.taps = bf16[24,128]{1,0:T(8,128)(2,1)} pad(bf16[19,19]{1,0:T(8,128)(2,1)} %param.7, bf16[]{:T(256)} %constant.5.clone.1), padding=0_5x0_109 | pad | bytes 6868 | tf_op jit(solution)/shard_map/jit(_pad)/pad | solution.py:382
  2.1 1.2 %reshape.70 = s32[128,1,288]{2,1,0:T(1,128)S(1)} reshape(s32[36864]{0:T(1024)} %param.10) | data formatting | bytes 294912 | tf_op jit(solution)/shard_map/reshape | solution.py:384
  3.3 1.2 %and_or_fusion.idx_ref = s32[128,1,384]{2,1,0:T(1,128)} fusion(pred[384]{0:T(512)(128)(4,1)S(1)} %fusion.4, s32[128,1,288]{2,1,0:T(1,128)S(1)} %reshape.70, s32[384]{0:T(512)S(1)} %get-tuple-element.12, s32[384]{0:T(512)S(1)} %get-tuple-element.13), kind=kLoop, calls=%fused_computation.4 | loop fusion | flops 491520 | bytes 347520 | tf_op jit(solution)/shard_map/or | solution.py:386
  4.5 1.5 %reshape.69 = s32[128,8,36]{2,1,0:T(8,128)S(1)} reshape(s32[36864]{0:T(1024)} %param.11) | data formatting | bytes 294912 | tf_op jit(solution)/shard_map/reshape | solution.py:388
  6.0 0.8 %pad.14.feet = s32[128,8,128]{2,1,0:T(8,128)} pad(s32[128,8,36]{2,1,0:T(8,128)S(1)} %reshape.69, s32[]{:T(128)} %constant.25.clone.1), padding=0_0x0_0x0_92 | pad | bytes 671748 | tf_op jit(solution)/shard_map/jit(_pad)/pad | solution.py:389
  6.9 0.0 copy-done
  6.9 2.5 %copy.19 = bf16[16,128,512]{2,0,1:T(8,128)(2,1)} copy(bf16[16,128,512]{2,1,0:T(8,128)(2,1)S(1)} %copy-done) | data formatting | bytes 4194304 | tf_op args[0]
  9.3 66.6 %collocate.1 = (bf16[128,16,512]{2,1,0:T(8,128)(2,1)}, f32[16,1536]{1,0:T(8,128)}) custom-call(bf16[128,16,512]{2,1,0:T(8,128)(2,1)} %bitcast.5, bf16[24,128]{1,0:T(8,128)(2,1)} %pad.12.taps, bf16[16,512]{1,0:T(8,128)(2,1)} %srf_ref.1, bf16[512,6144]{1,0:T(8,128)(2,1)} %spectra.1, s32[128,1,384]{2,1,0:T(1,128)} %and_or_fusion.idx_ref, s32[128,8,128]{2,1,0:T(8,128)} %pad.14.feet), custom_call_target="tpu_custom_call" | custom-call | flops 17179869184 | bytes 16777216 | tf_op jit(solution)/shard_map/collocate/pallas_call | solution.py:392
  75.9 0.0 copy-start.1
  75.9 4.1 %copy.17 = bf16[16,128,512]{2,1,0:T(8,128)(2,1)} copy(bf16[16,128,512]{2,0,1:T(8,128)(2,1)} %bitcast.4) | data formatting | bytes 4194304
  80.0 0.0 copy-done.1
  80.0 0.6 copy.21
  (2 shorter events, 0.0 us)
Async XLA Ops:
  0.6 6.2 %copy-start = (bf16[16,128,512]{2,1,0:T(8,128)(2,1)S(1)}, bf16[16,128,512]{2,1,0:T(8,128)(2,1)}, u32[]{:S(2)}) copy-start(bf16[16,128,512]{2,1,0:T(8,128)(2,1)} %param.6) | copy-start | bytes 6291460
  75.9 4.1 %copy-start.1 = (f32[16,1536]{1,0:T(8,128)S(1)}, f32[16,1536]{1,0:T(8,128)}, u32[]{:S(2)}) copy-start(f32[16,1536]{1,0:T(8,128)} %get-tuple-element.17) | copy-start | bytes 294916

commit v5 on v4

--- a/solution.py
+++ b/solution.py
@@ -24,7 +24,7 @@
 BATCH = 6
 SLOTS = 2 * BATCH
 TRIPS = 10
-LAG = 8
+LAG = 10
 TRIOS = 2 * (2 * TRIPS + 1)
 MESH = pl.DeviceIdType.MESH
 F32 = jnp.float32
@@ -138,10 +138,10 @@
     w_ref[0] = jnp.zeros((256, 128), BF16)
     w_ref[KS + 1] = jnp.zeros((256, 128), BF16)
 
-    tap = lax.broadcasted_iota(jnp.int32, (128, 256), 0)
-    at = lax.broadcasted_iota(jnp.int32, (128, 256), 1)
+    tap = lax.broadcasted_iota(jnp.int32, (KS, 256), 0)
+    at = lax.broadcasted_iota(jnp.int32, (KS, 256), 1)
     flip = jnp.where((tap + at == 256) | ((tap == 0) & (at == 0)), 1.0, 0.0).astype(BF16)
-    lines[...] = jnp.dot(taps[...], flip, preferred_element_type=F32)
+    lines[0:KS, :] = jnp.dot(taps[...], flip, preferred_element_type=F32)
 
     def band(a, carry):
         line = jnp.broadcast_to(lines[pl.ds(a, 1), :], (256, 256))
@@ -379,8 +379,6 @@
     hbm = pl.BlockSpec(memory_space=pl.ANY)
 
     turned = jnp.transpose(disk, (1, 0, 2))
-    taps = jnp.pad(response, ((0, 24 - KS), (0, 128 - KS)))
-
     pix = jnp.pad(send_pix.reshape(ND, 1, CAP), ((0, 0), (0, 0), (0, 384 - CAP)))
     slot = lax.broadcasted_iota(jnp.int32, pix.shape, 2) // ROWS
     idx = (((slot - (pix >> 9)) & 7) << 13) | ((pix >> 12) << 9) | (pix & 511)
@@ -435,7 +433,7 @@
         ),
         cost_estimate=pl.CostEstimate(flops=16 << 30, bytes_accessed=16 << 20, transcendentals=0),
         name="collocate",
-    )(turned, taps, srf, spectra, idx, foot)
+    )(turned, response, srf, spectra, idx, foot)
     return jnp.transpose(blurred, (1, 0, 2)), mismatch
 
 

time: 80.9 us -> 79.3 us (0.980)
  local copies, waits for them, and re-layouts: 12.2 us -> 11 us
    pad x1 -> x0, local copies, waits for them, and re-layouts: 1.44 us -> none  [body(): taps = jnp.pad(response, ((0, 24 - KS), (0, 128 - KS)))]
where the time goes in v5:
time: 79.3 us; the launch traced here: 79.1 us
  Pallas kernels  66.3 us (84%)
  local copies, waits for them, and re-layouts  11 us (14%)
  other arithmetic  1.18 us (1%)
    pallas_call x1, Pallas kernels, body(): pl.pallas_call(kernel, out_shape=(jax.ShapeDtypeStruct((TR, BANDS, TC), B...  66.3 us
    unnamed x7, local copies, waits for them, and re-layouts  7.23 us

profile of v5, /device:TPU:1, one launch (start us, length us, event | category | flops | bytes accessed | tf_op | source)
XLA Modules:
  0.0 79.1 jit_solution(5323274376892171246)
XLA Ops:
  0.6 0.0 copy-start
  0.7 1.3 %reshape.70 = s32[128,1,288]{2,1,0:T(1,128)S(1)} reshape(s32[36864]{0:T(1024)} %param.10) | data formatting | bytes 294912 | tf_op jit(solution)/shard_map/reshape | solution.py:382
  2.0 1.2 %and_or_fusion.idx_ref = s32[128,1,384]{2,1,0:T(1,128)} fusion(pred[384]{0:T(512)(128)(4,1)S(1)} %fusion.4, s32[128,1,288]{2,1,0:T(1,128)S(1)} %reshape.70, s32[384]{0:T(512)S(1)} %get-tuple-element.12, s32[384]{0:T(512)S(1)} %get-tuple-element.13), kind=kLoop, calls=%fused_computation.4 | loop fusion | flops 491520 | bytes 347520 | tf_op jit(solution)/shard_map/or | solution.py:384
  3.2 1.5 %reshape.69 = s32[128,8,36]{2,1,0:T(8,128)S(1)} reshape(s32[36864]{0:T(1024)} %param.11) | data formatting | bytes 294912 | tf_op jit(solution)/shard_map/reshape | solution.py:386
  4.7 0.8 %pad.9.feet = s32[128,8,128]{2,1,0:T(8,128)} pad(s32[128,8,36]{2,1,0:T(8,128)S(1)} %reshape.69, s32[]{:T(128)} %constant.23.clone.1), padding=0_0x0_0x0_92 | pad | bytes 671748 | tf_op jit(solution)/shard_map/jit(_pad)/pad | solution.py:387
  5.6 0.0 copy-done
  5.6 2.5 %copy.19 = bf16[16,128,512]{2,0,1:T(8,128)(2,1)} copy(bf16[16,128,512]{2,1,0:T(8,128)(2,1)S(1)} %copy-done) | data formatting | bytes 4194304 | tf_op args[0]
  8.0 66.3 %collocate.1 = (bf16[128,16,512]{2,1,0:T(8,128)(2,1)}, f32[16,1536]{1,0:T(8,128)}) custom-call(bf16[128,16,512]{2,1,0:T(8,128)(2,1)} %bitcast.5, bf16[19,19]{1,0:T(8,128)(2,1)} %taps.1, bf16[16,512]{1,0:T(8,128)(2,1)} %srf_ref.1, bf16[512,6144]{1,0:T(8,128)(2,1)} %spectra.1, s32[128,1,384]{2,1,0:T(1,128)} %and_or_fusion.idx_ref, s32[128,8,128]{2,1,0:T(8,128)} %pad.9.feet), custom_call_target="tpu_custom_call" | custom-call | flops 17179869184 | bytes 16777216 | tf_op jit(solution)/shard_map/collocate/pallas_call | solution.py:390
  74.3 0.0 copy-start.1
  74.3 4.1 %copy.17 = bf16[16,128,512]{2,1,0:T(8,128)(2,1)} copy(bf16[16,128,512]{2,0,1:T(8,128)(2,1)} %bitcast.4) | data formatting | bytes 4194304
  78.4 0.0 copy-done.1
  78.4 0.6 copy.21
  (2 shorter events, 0.0 us)
Async XLA Ops:
  0.6 4.9 %copy-start = (bf16[16,128,512]{2,1,0:T(8,128)(2,1)S(1)}, bf16[16,128,512]{2,1,0:T(8,128)(2,1)}, u32[]{:S(2)}) copy-start(bf16[16,128,512]{2,1,0:T(8,128)(2,1)} %param.6) | copy-start | bytes 6291460
  74.3 4.1 %copy-start.1 = (f32[16,1536]{1,0:T(8,128)S(1)}, f32[16,1536]{1,0:T(8,128)}, u32[]{:S(2)}) copy-start(f32[16,1536]{1,0:T(8,128)} %get-tuple-element.17) | copy-start | bytes 294916
